TPU v7x, 512 devices: a whole 4x4x16 slice. The times are simulated.
512 devices in a mesh: vox: 32 (over y, z_hi, x), chan: 16 (over z_lo, core).
Axes of the slice: x: 4, y: 4, z: 16 (z_hi: 2, z_lo: 8; z = z_hi * 8 + z_lo), core: 2. Of those that a mesh axis runs over, the one named last changes fastest.
Arguments:
- activations: bfloat16 [1024, 32, 512], P('chan', 'vox'), may hold values from -6 to 6
- upstream: bfloat16 [512, 32, 512], P('chan', 'vox'), may hold values from -6 to 6
- weights: bfloat16 [512, 27, 1024], P('chan'), may hold values from -0.0390625 to 0.0390625
Outputs:
- outputs: bfloat16 [512, 32, 512], P('chan', 'vox')
- input_grad: bfloat16 [1024, 32, 512], P('chan', 'vox')
- weight_grad: bfloat16 [512, 27, 1024], P('chan')
All inputs are finite; a program needn't handle non-finite values.
Results may differ from a plain program's by a relative error of at most 0.001.
Values may be sent and summed in bfloat16 or wider, within the bound.
No kernel may reach another device: no remote copies, remote signals or barrier semaphores. Data moves between devices by JAX's collectives and lax.ppermute only.
A program may use at most 128 MiB of HBM per device.

v0:
```python
import jax
import jax.numpy as jnp
from jax import lax
from jax.sharding import Mesh
from jax.sharding import PartitionSpec as P

NY = 32
NZ = 16
VOX = ("vox_0", "vox_1", "vox_2")
CHAN = ("chan_0", "chan_1")


tap_offsets = [(a, b, c) for a in (-1, 0, 1) for b in (-1, 0, 1) for c in (-1, 0, 1)]


def padded_2(value, sides, width):
    for axis, dim in sides:
        size, length = (lax.axis_size(axis), value.shape[dim])
        up = [(i, (i + 1) % size) for i in range(size - 1)]
        down = [(j, i) for i, j in up]
        last = lax.slice_in_dim(value, length - width, length, axis=dim)
        leading = lax.slice_in_dim(value, 0, width, axis=dim)
        before = lax.ppermute(last, axis, up)
        after = lax.ppermute(leading, axis, down)
        value = jnp.concatenate([before, value, after], axis=dim)
    return value


def sent_to_all(value, axis):
    copies = jnp.broadcast_to(value, (lax.axis_size(axis), *value.shape))
    return lax.all_to_all(copies, axis, split_axis=0, concat_axis=0, tiled=True)


def laid_out(pieces, dim):
    pieces = jnp.moveaxis(pieces, 0, dim)
    dims = pieces.shape
    return pieces.reshape(*dims[:dim], dims[dim] * dims[dim + 1], *dims[dim + 2 :])


def gathered_by_axis(value, axes, dim):
    far, near = axes
    pieces = sent_to_all(sent_to_all(value, far), near)
    return laid_out(pieces.swapaxes(0, 1).reshape(-1, *value.shape), dim)


def padded_to(lines, size):
    spare = -len(lines) % size
    return jnp.pad(lines, [(0, spare)] + [(0, 0)] * (lines.ndim - 1))


def in_blocks(value, dim, size):
    before, after = (value.shape[:dim], value.shape[dim + 1 :])
    return jnp.moveaxis(value.reshape(*before, size, -1, *after), dim, 0)


def summed_on_arrival(value, axis, dim):
    size = lax.axis_size(axis)
    pieces = lax.all_to_all(in_blocks(value, dim, size), axis, 0, 0, tiled=True)
    return jnp.sum(pieces, axis=0)


def sum_by_axis(value, axes, dim):
    far, near = axes
    own = summed_on_arrival(in_blocks(value, dim, lax.axis_size(far)), near, dim + 1)
    return jnp.sum(lax.all_to_all(own, far, 0, 0, tiled=True), axis=0)


def nested_sum(value, axes):
    lines = value.reshape(-1, value.shape[-1])
    padded = padded_to(lines, lax.axis_size(axes[0]) * lax.axis_size(axes[1]))
    whole = gathered_by_axis(sum_by_axis(padded, axes, 0), axes, 0)
    return lax.slice_in_dim(whole, 0, len(lines)).reshape(value.shape)


def spread(slab_in, orient):
    channels = slab_in.shape[0]
    planes = slab_in.shape[1] - 2
    width = slab_in.shape[2]
    lane = lax.iota(jnp.int32, width) % NZ
    padded = jnp.pad(slab_in, ((0, 0), (0, 0), (NZ + 1, NZ + 1)))
    columns = []
    for offsets in tap_offsets:
        off_x = orient * offsets[0]
        off_y = orient * offsets[1]
        off_z = orient * offsets[2]
        start = NZ + 1 + off_y * NZ + off_z
        window = padded[:, 1 + off_x : 1 + off_x + planes, start : start + width]
        if off_z == -1:
            window = jnp.where(lane >= 1, window, jnp.zeros_like(window))
        elif off_z == 1:
            window = jnp.where(lane <= NZ - 2, window, jnp.zeros_like(window))
        columns.append(window.reshape(channels, planes * width))
    return jnp.stack(columns, axis=0)


def local(activations, upstream, weights):
    cin_dev = activations.shape[0]
    cout_dev = upstream.shape[0]
    slab_x = activations.shape[1]
    voxels = slab_x * NY * NZ
    x_halo = padded_2(activations, ((VOX, 1),), 1)
    up_flat = upstream.reshape(cout_dev, voxels)
    panel = gathered_by_axis(x_halo, ("chan_0", "chan_1"), 0)
    panel_rows = panel.shape[0]
    columns = spread(panel, 1).reshape(27 * panel_rows, voxels)
    w_panel = weights.reshape(cout_dev, 27 * panel_rows)
    out_total = jnp.dot(w_panel, columns, preferred_element_type=jnp.float32)
    grad_term = lax.dot_general(
        up_flat, columns, (((1,), (1,)), ((), ())), preferred_element_type=jnp.float32
    )
    grad_total = grad_term.reshape(cout_dev, 27, panel_rows)
    out_total, grad_local = (out_total, grad_total)
    outputs = out_total.reshape(cout_dev, slab_x, NY * NZ).astype(jnp.bfloat16)
    grad_scale = 1.0 / jnp.sqrt(jnp.float32(slab_x * lax.axis_size(VOX) * NY * NZ))
    grad_whole = nested_sum(grad_local, (("vox_0", "vox_1"), "vox_2"))
    weight_grad = (grad_whole * grad_scale).astype(jnp.bfloat16)
    dy_halo = padded_2(upstream, ((VOX, 1),), 1)
    back_columns = spread(dy_halo, -1)
    partial_grad = jnp.einsum(
        "okc,kov->cv", weights, back_columns, preferred_element_type=jnp.float32
    )
    grad_sum = summed_on_arrival(
        partial_grad.reshape(cin_dev * lax.axis_size(CHAN), slab_x, NY * NZ), CHAN, 0
    )
    input_grad = grad_sum.astype(jnp.bfloat16)
    return (outputs, input_grad, weight_grad)


def solution(mesh):
    finer = Mesh(
        mesh.devices.reshape(4, 2, 4, 8, 2), ("vox_0", "vox_1", "vox_2", "chan_0", "chan_1")
    )
    in_specs = (P(CHAN, VOX, None), P(CHAN, VOX, None), P(CHAN, None, None))
    out_specs = (P(CHAN, VOX, None), P(CHAN, VOX, None), P(CHAN, None, None))
    return jax.shard_map(local, mesh=finer, in_specs=in_specs, out_specs=out_specs, check_vma=False)
```

profile of v0, /device:TPU:96, one launch (start us, length us, event | category | flops | bytes accessed | tf_op | source)
XLA Modules:
  0.0 488.0 jit_solution(11877300711848175206)
XLA Ops:
  0.6 3.5 collective-permute-start
  6.4 4.2 collective-permute-done.1
  12.7 11.7 %all-to-all-start = ((bf16[8,64,3,512]{3,1,2,0:T(8,128)(2,1)}), bf16[8,64,3,512]{3,1,2,0:T(8,128)(2,1)S(1)}, u32[]{:S(2)}, u32[]{:S(2)}) async-start(bf16[8,64,3,512]{3,1,2,0:T(8,128)(2,1)} %broadcast_in_dim.123), calls=%async_computation | async-start | bytes 3145728 | tf_op jit(solution)/shard_map/all_to_all | solution.py:31
  24.5 68.6 %all-to-all-done = bf16[8,64,3,512]{3,1,2,0:T(8,128)(2,1)S(1)} async-done(((bf16[8,64,3,512]{3,1,2,0:T(8,128)(2,1)}), bf16[8,64,3,512]{3,1,2,0:T(8,128)(2,1)S(1)}, u32[]{:S(2)}, u32[]{:S(2)}) %all-to-all-start) | async-done | bytes 1572896 | tf_op jit(solution)/shard_map/all_to_all | solution.py:31
  93.6 6.3 %all_to_all.35 = bf16[2,8,64,3,512]{4,2,1,3,0:T(8,128)(2,1)S(1)} all-to-all(bf16[2,8,64,3,512]{4,2,1,3,0:T(8,128)(2,1)S(1)} %broadcast_in_dim.124), channel_id=1, replica_groups=mesh['vox_0'=4,'vox_1'=2,'vox_2'=4,'chan_0'=8,'chan_1'=2] {'chan_1'}, dimensions={0} | all-to-all | bytes 6291456 | tf_op jit(solution)/shard_map/all_to_all | solution.py:31
  112.9 9.3 %copy-done.1 = bf16[27,1024,512]{2,1,0:T(8,128)(2,1)} copy-done((bf16[27,1024,512]{2,1,0:T(8,128)(2,1)}, bf16[27,1024,512]{2,1,0:T(8,128)(2,1)S(1)}, u32[]{:S(2)}) %copy-start.1) | copy-done | bytes 28311576
  122.2 15.2 %convolution_bitcast_fusion = f32[32,27648]{1,0:T(8,128)} fusion(bf16[27648,512]{1,0:T(8,128)(2,1)} %bitcast.275, bf16[32,1,512]{2,0,1:T(8,128)(2,1)S(1)} %copy-done.2), kind=kOutput, calls=%fused_computation | convolution fusion | flops 905969664 | bytes 31883264 | tf_op jit(solution)/shard_map/dot_general | solution.py:108
  137.4 3.9 reshape_reshape.12
  141.3 6.0 %copy.31 = f32[4,8,27,1024]{3,1,2,0:T(8,128)} copy(f32[4,8,27,1024]{3,2,0,1:T(8,128)} %bitcast.276) | data formatting | bytes 7077888 | tf_op jit(solution)/shard_map/transpose | solution.py:53
  147.3 16.7 %all-to-all-start.3 = ((f32[4,8,27,1024]{3,1,2,0:T(8,128)}), f32[4,8,27,1024]{3,1,2,0:T(8,128)}, u32[]{:S(2)}, u32[]{:S(2)}) async-start(f32[4,8,27,1024]{3,1,2,0:T(8,128)} %copy.31), calls=%async_computation.3 | async-start | bytes 7077888 | tf_op jit(solution)/shard_map/all_to_all | solution.py:58
  164.0 3.9 collective-permute-start.2
  169.2 33.9 %collective-permute-done.2 = bf16[32,1,512]{2,0,1:T(8,128)(2,1)S(1)} collective-permute-done((bf16[32,1,512]{2,0,1:T(8,128)(2,1)S(1)}, bf16[32,1,512]{2,0,1:T(8,128)(2,1)S(1)}, u32[]{:S(2)}, u32[]{:S(2)}) %collective-permute-start.2) | collective-permute-done | bytes 32800 | tf_op jit(solution)/shard_map/ppermute | solution.py:23
  211.4 12.7 %all-to-all-start.4 = ((f32[8,27,1024]{2,1,0:T(8,128)}), f32[8,27,1024]{2,1,0:T(8,128)S(1)}, u32[]{:S(2)}, u32[]{:S(2)}) async-start(f32[8,27,1024]{2,1,0:T(8,128)} %copy.32), calls=%async_computation.4 | async-start | bytes 2097152 | tf_op jit(solution)/shard_map/all_to_all | solution.py:65
  233.5 65.3 %all-to-all-done.4 = f32[8,27,1024]{2,1,0:T(8,128)S(1)} async-done(((f32[8,27,1024]{2,1,0:T(8,128)}), f32[8,27,1024]{2,1,0:T(8,128)S(1)}, u32[]{:S(2)}, u32[]{:S(2)}) %all-to-all-start.4) | async-done | bytes 884768 | tf_op jit(solution)/shard_map/all_to_all | solution.py:65
  300.0 3.6 all-to-all-start.5
  311.0 3.9 convolution_bitcast_fusion.1
  314.8 2.9 copy.29
  317.7 14.9 %all-to-all-done.5 = f32[8,27,1024]{2,1,0:T(8,128)S(1)} async-done(((f32[8,27,1024]{2,1,0:T(8,128)}), f32[8,27,1024]{2,1,0:T(8,128)S(1)}, u32[]{:S(2)}, u32[]{:S(2)}) %all-to-all-start.5) | async-done | bytes 884768 | tf_op jit(solution)/shard_map/all_to_all | solution.py:31
  332.6 5.1 %all-to-all-start.2 = ((f32[16,64,1,512]{3,1,2,0:T(8,128)}), f32[16,64,1,512]{3,1,2,0:T(8,128)}, u32[]{:S(2)}, u32[]{:S(2)}) async-start(f32[16,64,1,512]{3,1,2,0:T(8,128)} %bitcast.278), calls=%async_computation.2 | async-start | bytes 4194304 | tf_op jit(solution)/shard_map/all_to_all | solution.py:58
  339.2 92.0 %all-to-all-done.2 = f32[16,64,1,512]{3,1,2,0:T(8,128)} async-done(((f32[16,64,1,512]{3,1,2,0:T(8,128)}), f32[16,64,1,512]{3,1,2,0:T(8,128)}, u32[]{:S(2)}, u32[]{:S(2)}) %all-to-all-start.2) | async-done | bytes 2097184 | tf_op jit(solution)/shard_map/all_to_all | solution.py:58
  431.1 3.4 broadcast_in_dim.129
  434.5 5.0 %all-to-all-start.6 = ((f32[4,8,27,1024]{3,1,2,0:T(8,128)}), f32[4,8,27,1024]{3,1,2,0:T(8,128)}, u32[]{:S(2)}, u32[]{:S(2)}) async-start(f32[4,8,27,1024]{3,1,2,0:T(8,128)} %broadcast_in_dim.129), calls=%async_computation.6 | async-start | bytes 7077888 | tf_op jit(solution)/shard_map/all_to_all | solution.py:31
  439.5 12.2 %fusion.2 = bf16[32,1,512]{2,0,1:T(8,128)(2,1)} fusion(bf16[32,27,1024]{2,0,1:T(8,128)(2,1)S(1)} %copy-done, bf16[27,1024,512]{2,1,0:T(8,128)(2,1)} %copy-done.1), kind=kOutput, calls=%fused_computation.30 | convolution fusion | flops 905986048 | bytes 30113792 | tf_op jit(solution)/shard_map/dot_general | solution.py:107
  454.1 27.9 %all-to-all-done.6 = f32[4,8,27,1024]{3,1,2,0:T(8,128)} async-done(((f32[4,8,27,1024]{3,1,2,0:T(8,128)}), f32[4,8,27,1024]{3,1,2,0:T(8,128)}, u32[]{:S(2)}, u32[]{:S(2)}) %all-to-all-start.6) | async-done | bytes 3538976 | tf_op jit(solution)/shard_map/all_to_all | solution.py:31
  (81 shorter events, 55.1 us)
Async XLA Ops:
  0.6 310.3 %copy-start = (bf16[32,27,1024]{2,0,1:T(8,128)(2,1)S(1)}, bf16[32,27,1024]{2,0,1:T(8,128)(2,1)}, u32[]{:S(2)}) copy-start(bf16[32,27,1024]{2,0,1:T(8,128)(2,1)} %param.5) | copy-start | bytes 5308420
  0.6 5.7 %collective-permute-start = (bf16[64,1,512]{2,0,1:T(8,128)(2,1)}, bf16[64,1,512]{2,0,1:T(8,128)(2,1)S(1)}, u32[]{:S(2)}, u32[]{:S(2)}) collective-permute-start(bf16[64,1,512]{2,0,1:T(8,128)(2,1)} %param.3), channel_id=1, source_target_pairs={{0,16},{16,32},{32,48},{48,64},{64,80},{80,96},{96,112},{112,128},... | collective-permute-start | bytes 196616 | tf_op jit(solution)/shard_map/ppermute | solution.py:23
  4.2 6.4 %collective-permute-start.1 = (bf16[64,1,512]{2,0,1:T(8,128)(2,1)}, bf16[64,1,512]{2,0,1:T(8,128)(2,1)S(1)}, u32[]{:S(2)}, u32[]{:S(2)}) collective-permute-start(bf16[64,1,512]{2,0,1:T(8,128)(2,1)} %param.3), channel_id=1, source_target_pairs={{16,0},{32,16},{48,32},{64,48},{80,64},{96,80},{112,96},{128,112},... | collective-permute-start | bytes 196616 | tf_op jit(solution)/shard_map/ppermute | solution.py:24
  12.7 80.3 %all-to-all-start = ((bf16[8,64,3,512]{3,1,2,0:T(8,128)(2,1)}), bf16[8,64,3,512]{3,1,2,0:T(8,128)(2,1)S(1)}, u32[]{:S(2)}, u32[]{:S(2)}) async-start(bf16[8,64,3,512]{3,1,2,0:T(8,128)(2,1)} %broadcast_in_dim.123), calls=%async_computation | async-start | bytes 3145728 | tf_op jit(solution)/shard_map/all_to_all | solution.py:31
  106.4 15.8 %copy-start.2 = (bf16[32,1,512]{2,0,1:T(8,128)(2,1)S(1)}, bf16[32,1,512]{2,0,1:T(8,128)(2,1)}, u32[]{:S(2)}) copy-start(bf16[32,1,512]{2,0,1:T(8,128)(2,1)} %param.4) | copy-start | bytes 98308
  112.9 9.3 %copy-start.1 = (bf16[27,1024,512]{2,1,0:T(8,128)(2,1)}, bf16[27,1024,512]{2,1,0:T(8,128)(2,1)S(1)}, u32[]{:S(2)}) copy-start(bf16[27,1024,512]{2,1,0:T(8,128)(2,1)S(1)} %fusion.68) | copy-start | bytes 84934656
  147.3 60.1 %all-to-all-start.3 = ((f32[4,8,27,1024]{3,1,2,0:T(8,128)}), f32[4,8,27,1024]{3,1,2,0:T(8,128)}, u32[]{:S(2)}, u32[]{:S(2)}) async-start(f32[4,8,27,1024]{3,1,2,0:T(8,128)} %copy.31), calls=%async_computation.3 | async-start | bytes 7077888 | tf_op jit(solution)/shard_map/all_to_all | solution.py:58
  164.0 39.1 %collective-permute-start.2 = (bf16[32,1,512]{2,0,1:T(8,128)(2,1)S(1)}, bf16[32,1,512]{2,0,1:T(8,128)(2,1)S(1)}, u32[]{:S(2)}, u32[]{:S(2)}) collective-permute-start(bf16[32,1,512]{2,0,1:T(8,128)(2,1)S(1)} %copy-done.2), channel_id=1, source_target_pairs={{0,16},{16,32},{32,48},{48,64},{64,80},{80,96},{96,112},{112,128},... | collective-permute-start | bytes 98312 | tf_op jit(solution)/shard_map/ppermute | solution.py:23
  167.9 38.0 %collective-permute-start.3 = (bf16[32,1,512]{2,0,1:T(8,128)(2,1)S(1)}, bf16[32,1,512]{2,0,1:T(8,128)(2,1)S(1)}, u32[]{:S(2)}, u32[]{:S(2)}) collective-permute-start(bf16[32,1,512]{2,0,1:T(8,128)(2,1)S(1)} %copy-done.2), channel_id=1, source_target_pairs={{16,0},{32,16},{48,32},{64,48},{80,64},{96,80},{112,96},{128,112},... | collective-permute-start | bytes 98312 | tf_op jit(solution)/shard_map/ppermute | solution.py:24
  211.4 87.5 %all-to-all-start.4 = ((f32[8,27,1024]{2,1,0:T(8,128)}), f32[8,27,1024]{2,1,0:T(8,128)S(1)}, u32[]{:S(2)}, u32[]{:S(2)}) async-start(f32[8,27,1024]{2,1,0:T(8,128)} %copy.32), calls=%async_computation.4 | async-start | bytes 2097152 | tf_op jit(solution)/shard_map/all_to_all | solution.py:65
  300.0 32.6 %all-to-all-start.5 = ((f32[8,27,1024]{2,1,0:T(8,128)}), f32[8,27,1024]{2,1,0:T(8,128)S(1)}, u32[]{:S(2)}, u32[]{:S(2)}) async-start(f32[8,27,1024]{2,1,0:T(8,128)} %broadcast_in_dim.128), calls=%async_computation.5 | async-start | bytes 2097152 | tf_op jit(solution)/shard_map/all_to_all | solution.py:31
  332.6 98.5 %all-to-all-start.2 = ((f32[16,64,1,512]{3,1,2,0:T(8,128)}), f32[16,64,1,512]{3,1,2,0:T(8,128)}, u32[]{:S(2)}, u32[]{:S(2)}) async-start(f32[16,64,1,512]{3,1,2,0:T(8,128)} %bitcast.278), calls=%async_computation.2 | async-start | bytes 4194304 | tf_op jit(solution)/shard_map/all_to_all | solution.py:58
  434.5 47.4 %all-to-all-start.6 = ((f32[4,8,27,1024]{3,1,2,0:T(8,128)}), f32[4,8,27,1024]{3,1,2,0:T(8,128)}, u32[]{:S(2)}, u32[]{:S(2)}) async-start(f32[4,8,27,1024]{3,1,2,0:T(8,128)} %broadcast_in_dim.129), calls=%async_computation.6 | async-start | bytes 7077888 | tf_op jit(solution)/shard_map/all_to_all | solution.py:31
where the time goes:
time: 489 us; the launch traced here: 488 us
  waiting for transfers between devices  310 us (63%)
  starting transfers between devices  64.8 us (13%)
  local copies, waits for them, and re-layouts  44.3 us (9%)
  matrix products  31.3 us (6%)
  other arithmetic  30 us (6%)
  blocking collectives  6.26 us (1%)
    all_to_all x3, waiting for transfers between devices, sent_to_all(): return lax.all_to_all(copies, axis, split_axis=0, concat_axis=0, tiled=True)  111 us
    all_to_all x2, waiting for transfers between devices, summed_on_arrival(): pieces = lax.all_to_all(in_blocks(value, dim, size), axis, 0, 0, tiled=True)  92 us
    all_to_all x1, waiting for transfers between devices, sum_by_axis(): return jnp.sum(lax.all_to_all(own, far, 0, 0, tiled=True), axis=0)  65.3 us
    ppermute x2, waiting for transfers between devices, padded_2(): before = lax.ppermute(last, axis, up)  34.8 us
    all_to_all x2, starting transfers between devices, summed_on_arrival(): pieces = lax.all_to_all(in_blocks(value, dim, size), axis, 0, 0, tiled=True)  21.8 us
    unnamed x34, other arithmetic  20.5 us
    all_to_all x3, starting transfers between devices, sent_to_all(): return lax.all_to_all(copies, axis, split_axis=0, concat_axis=0, tiled=True)  20.2 us
    unnamed x24, local copies, waits for them, and re-layouts  18.5 us
  transfers between devices with their start and end apart: 10, of which 9 were waited for; matrix products, arithmetic and copies ran while one was open for 8% of the time, Pallas kernels for 0%

commit v1 on v0

v1 whole, which is shorter than its diff:
```python
import functools

import jax
import jax.numpy as jnp
from jax import lax
from jax.experimental import pallas as pl
from jax.experimental.pallas import tpu as pltpu
from jax.sharding import Mesh
from jax.sharding import PartitionSpec as P


NY = 32
NZ = 16
PLANE = NY * NZ
VOX = ("y", "zh", "x")
XY = ("y", "x")
CHAN = ("zl", "co")
F32 = jnp.float32
BF16 = jnp.bfloat16


def moved(value, b, c):
    step = NZ * b + c
    if step == 0:
        return value
    out = pltpu.roll(value, (-step) % PLANE, 1)
    lane = lax.broadcasted_iota(jnp.int32, value.shape, 1)
    keep = None
    if b != 0:
        keep = (lane + NZ * b >= 0) & (lane + NZ * b < PLANE)
    if c != 0:
        col = lane % NZ + c
        inside = (col >= 0) & (col < NZ)
        keep = inside if keep is None else keep & inside
    return jnp.where(keep, out, 0.0)


def forward_kernel(w_ref, x_ref, o_ref, x_rows):
    rows = o_ref.shape[1]
    cores, chips, ch = x_ref.shape[:3]
    for z in range(chips):
        for e in range(cores):
            first = (z * cores + e) * ch
            x_rows[first : first + ch, :] = x_ref[e, z]
    for a in range(3):
        y = jnp.dot(w_ref[9 * rows * a : 9 * rows * (a + 1), :], x_rows[...], preferred_element_type=F32)
        total = None
        for b in range(3):
            for c in range(3):
                k = 3 * b + c
                term = moved(y[rows * k : rows * (k + 1), :], b - 1, c - 1)
                total = term if total is None else total + term
        o_ref[a] = total


def forward(w_rows, x):
    rows = w_rows.shape[0] // 27
    return pl.pallas_call(
        forward_kernel,
        out_shape=jax.ShapeDtypeStruct((3, rows, PLANE), F32),
        scratch_shapes=[pltpu.VMEM((w_rows.shape[1], PLANE), BF16)],
        compiler_params=pltpu.CompilerParams(vmem_limit_bytes=32 * 2**20),
        name="forward_plane",
    )(w_rows, x)


def backward_kernel(w_ref, u_ref, o_ref, cols):
    rows = u_ref.shape[1]
    for a in range(3):
        plane = u_ref[2 - a].astype(F32)
        for b in range(3):
            for c in range(3):
                k = 9 * a + 3 * b + c
                cols[rows * k : rows * (k + 1), :] = moved(plane, 1 - b, 1 - c).astype(BF16)
    ch = o_ref.shape[2]
    cores = o_ref.shape[0]
    for z in range(o_ref.shape[1]):
        part = w_ref[:, ch * cores * z : ch * cores * (z + 1)]
        got = lax.dot_general(part, cols[...], (((0,), (0,)), ((), ())), preferred_element_type=F32)
        for e in range(cores):
            o_ref[e, z] = got[ch * e : ch * (e + 1)]


def backward(w_rows, planes, cores, chips):
    width = w_rows.shape[1]
    rows = planes.shape[1]
    return pl.pallas_call(
        backward_kernel,
        out_shape=jax.ShapeDtypeStruct((cores, chips, width // (cores * chips), PLANE), F32),
        scratch_shapes=[pltpu.VMEM((27 * rows, PLANE), BF16)],
        compiler_params=pltpu.CompilerParams(vmem_limit_bytes=32 * 2**20),
        name="backward_plane",
    )(w_rows, planes)


def filter_kernel(a_ref, u_ref, o_ref, lhs, rhs, acc):
    run, chans = a_ref.shape[0], a_ref.shape[1]
    rows = u_ref.shape[2]

    @pl.when(pl.program_id(0) == 0)
    def _():
        acc[...] = jnp.zeros_like(acc)

    for q in range(run + 2):
        if q == 0:
            plane = u_ref[0, 1]
        elif q == run + 1:
            plane = u_ref[run - 1, 1]
        else:
            plane = u_ref[q - 1, 0]
        plane = plane.astype(F32)
        for c in range(3):
            lhs[q, rows * c : rows * (c + 1), :] = moved(plane, 0, 1 - c).astype(BF16)
    for q in range(run):
        plane = a_ref[q].astype(F32)
        for b in range(3):
            rhs[q, chans * b : chans * (b + 1), :] = moved(plane, b - 1, 0).astype(BF16)
    total = acc[...]
    for q in range(run):
        left = lhs[q : q + 3].reshape(9 * rows, PLANE)
        total = total + lax.dot_general(left, rhs[q], (((1,), (1,)), ((), ())), preferred_element_type=F32)
    acc[...] = total

    @pl.when(pl.program_id(0) == pl.num_programs(0) - 1)
    def _():
        low = lax.broadcasted_iota(jnp.int32, (8, 128), 1) < 64
        for k in range(27):
            a, b, c = k // 9, k // 3 % 3, k % 3
            for h in range(o_ref.shape[0]):
                row = rows * (3 * (2 - a) + c) + 16 * h
                if b == 2:
                    one = total[row : row + 8, 128:192]
                    two = total[row + 8 : row + 16, 128:192]
                    o_ref[h, k] = jnp.concatenate([one, two], axis=1)
                else:
                    one = total[row : row + 8, 0:128]
                    two = total[row + 8 : row + 16, 0:128]
                    if b == 0:
                        two = pltpu.roll(two, 64, 1)
                    else:
                        one = pltpu.roll(one, 64, 1)
                    o_ref[h, k] = jnp.where(low, one, two)


def filter_grad(acts, ups, runs):
    planes, chans = acts.shape[0], acts.shape[1]
    rows = ups.shape[2]
    run = planes // runs
    return pl.pallas_call(
        filter_kernel,
        grid=(runs,),
        in_specs=[
            pl.BlockSpec((run, chans, PLANE), lambda r: (r, 0, 0)),
            pl.BlockSpec((run, 2, rows, PLANE), lambda r: (r, 0, 0, 0)),
        ],
        out_specs=pl.BlockSpec((rows // 16, 27, 8, 128), lambda r: (0, 0, 0, 0)),
        out_shape=jax.ShapeDtypeStruct((rows // 16, 27, 8, 128), F32),
        scratch_shapes=[
            pltpu.VMEM((run + 2, 3 * rows, PLANE), BF16),
            pltpu.VMEM((run, 3 * chans, PLANE), BF16),
            pltpu.VMEM((9 * rows, 3 * chans), F32),
        ],
        compiler_params=pltpu.CompilerParams(vmem_limit_bytes=32 * 2**20),
        name="filter_planes",
    )(acts, ups)


def join_kernel(r_ref, o_ref, *, order):
    low = lax.broadcasted_iota(jnp.int32, (8, 128), 1) < 64
    for k in range(o_ref.shape[0]):
        for t in range(len(order) // 2):
            for h in range(r_ref.shape[1]):
                left = r_ref[order[2 * t], h, k].astype(F32)
                right = r_ref[order[2 * t + 1], h, k].astype(F32)
                one = jnp.where(low, left, pltpu.roll(right, 64, 1))
                two = jnp.where(low, pltpu.roll(left, 64, 1), right)
                both = jnp.concatenate([one, two], axis=0).astype(BF16)
                o_ref[k, 16 * h : 16 * (h + 1), 128 * t : 128 * (t + 1)] = both


def join(pieces, order):
    size, halves = pieces.shape[:2]
    return pl.pallas_call(
        functools.partial(join_kernel, order=order),
        grid=(9,),
        in_specs=[pl.BlockSpec((size, halves, 3, 8, 128), lambda g: (0, 0, g, 0, 0))],
        out_specs=pl.BlockSpec((3, 16 * halves, 64 * size), lambda g: (g, 0, 0)),
        out_shape=jax.ShapeDtypeStruct((27, 16 * halves, 64 * size), BF16),
        name="join_pieces",
    )(pieces)


def exchange(pieces, axes):
    return lax.all_to_all(pieces, axes, 0, 0, tiled=True)


def shared(value, axes):
    return exchange(jnp.broadcast_to(value, (lax.axis_size(axes), *value.shape)), axes)


def local(activations, upstream, weights):
    ch, co = activations.shape[0], upstream.shape[0]
    n_vox, n_x, n_y = lax.axis_size(VOX), lax.axis_size("x"), lax.axis_size("y")
    n_zl, n_co = lax.axis_size("zl"), lax.axis_size("co")
    n_xy = n_x * n_y
    cin = ch * n_zl * n_co
    up = [(i, i + 1) for i in range(n_vox - 1)]
    down = [(i + 1, i) for i in range(n_vox - 1)]
    act = activations.reshape(ch, PLANE)
    ups = upstream.reshape(co, PLANE)

    near = shared(act, "zl")

    before = lax.ppermute(ups, VOX, up)
    after = lax.ppermute(ups, VOX, down)
    edge = jnp.where(lax.axis_index("x") == 0, before, after)
    up_planes = jnp.stack([ups, edge])
    up_planes = lax.all_gather(up_planes, XY, axis=0, tiled=False)

    w_rows = weights.transpose(1, 0, 2).reshape(27 * co, cin)
    part = backward(w_rows, jnp.stack([before, ups, after]), n_co, n_zl)
    part = exchange(part, "co")
    part = jnp.sum(part, axis=0)
    part = lax.psum_scatter(part.reshape(n_zl * ch, PLANE), "zl", scatter_dimension=0, tiled=True)
    input_grad = part.astype(BF16).reshape(ch, 1, PLANE)

    plane = shared(near, "co")

    acts = exchange(plane.reshape(n_xy, ch, PLANE), XY)
    around = forward(w_rows, plane)
    from_after = lax.ppermute(around[2], VOX, down)
    from_before = lax.ppermute(around[0], VOX, up)
    outputs = (around[1] + from_after + from_before).astype(BF16).reshape(co, 1, PLANE)

    raw = filter_grad(acts, up_planes, n_y)
    raw = exchange(raw, "zh")
    raw = jnp.sum(raw, axis=0)
    scale = 1.0 / jnp.sqrt(jnp.float32(n_vox * PLANE))
    mine = (raw * scale).astype(BF16)
    halves = shared(mine, "zh")
    pieces = shared(halves, XY)
    order = tuple(e * n_zl + z for z in range(n_zl) for e in range(n_co))
    weight_grad = join(pieces, order).transpose(1, 0, 2)
    return (outputs, input_grad, weight_grad)


def solution(mesh):
    finer = Mesh(mesh.devices.reshape(SPLIT), ("y", "zh", "x", "zl", "co"))
    specs = (P(CHAN, VOX, None), P(CHAN, VOX, None), P(CHAN, None, None))

    return jax.shard_map(local, mesh=finer, in_specs=specs, out_specs=specs, check_vma=False)


SPLIT = (4, 2, 4, 8, 2)
```

time: 489 us -> 221 us (0.45)
  the two profiles are of different devices: /device:TPU:96 before, /device:TPU:24 now
where the time goes in v1:
time: 221 us; the launch traced here: 220 us
  waiting for transfers between devices  83.3 us (38%)
  starting transfers between devices  72.2 us (33%)
  blocking collectives  22.1 us (10%)
  between operations  15.6 us (7%)
  Pallas kernels  14.9 us (7%)
  other arithmetic  5.72 us (3%)
  local copies, waits for them, and re-layouts  5.7 us (3%)
    all_to_all x5, starting transfers between devices, exchange(): return lax.all_to_all(pieces, axes, 0, 0, tiled=True)  42.1 us
    all_to_all x5, waiting for transfers between devices, exchange(): return lax.all_to_all(pieces, axes, 0, 0, tiled=True)  26.2 us
    all_gather x1, waiting for transfers between devices, local(): up_planes = lax.all_gather(up_planes, XY, axis=0, tiled=False)  24.9 us
    all_to_all x2, blocking collectives, exchange(): return lax.all_to_all(pieces, axes, 0, 0, tiled=True)  22.1 us
    ppermute x1, waiting for transfers between devices, local(): before = lax.ppermute(ups, VOX, up)  16 us
    ppermute x1, starting transfers between devices, local(): from_after = lax.ppermute(around[2], VOX, down)  14.2 us
    reduce_scatter x1, waiting for transfers between devices, local(): lax.psum_scatter(part.reshape(n_zl * ch, PLANE), 'zl', scatter_dimension=...  12.4 us
    ppermute x1, starting transfers between devices, local(): after = lax.ppermute(ups, VOX, down)  10.6 us
  transfers between devices with their start and end apart: 11, of which 8 were waited for; matrix products, arithmetic and copies ran while one was open for 3% of the time, Pallas kernels for 4%

profile of v1, /device:TPU:24, one launch (start us, length us, event | category | flops | bytes accessed | tf_op | source)
XLA Modules:
  0.0 219.6 jit_solution(10162123654464117468)
XLA Ops:
  9.7 12.5 %all-to-all-start = ((bf16[8,64,512]{2,1,0:T(8,128)(2,1)}), bf16[8,64,512]{2,1,0:T(8,128)(2,1)S(1)}, u32[]{:S(2)}, u32[]{:S(2)}) async-start(bf16[8,64,512]{2,1,0:T(8,128)(2,1)} %broadcast_in_dim.12), calls=%async_computation | async-start | bytes 1048576 | tf_op jit(solution)/shard_map/all_to_all | solution.py:194
  22.3 10.6 %collective-permute-start.3 = (bf16[32,512]{1,0:T(8,128)(2,1)}, bf16[32,512]{1,0:T(8,128)(2,1)S(1)}, u32[]{:S(2)}, u32[]{:S(2)}) collective-permute-start(bf16[32,512]{1,0:T(8,128)(2,1)} %bitcast.39), channel_id=1, source_target_pairs={{16,0},{32,16},{48,32},{64,48},{80,64},{96,80},{112,96},{128,112},... | collective-permute-start | bytes 98312 | tf_op jit(solution)/shard_map/ppermute | solution.py:215
  32.9 1.9 collective-permute-start.2
  34.8 16.0 %collective-permute-done.2 = bf16[32,512]{1,0:T(8,128)(2,1)S(1)} collective-permute-done((bf16[32,512]{1,0:T(8,128)(2,1)}, bf16[32,512]{1,0:T(8,128)(2,1)S(1)}, u32[]{:S(2)}, u32[]{:S(2)}) %collective-permute-start.2) | collective-permute-done | bytes 32800 | tf_op jit(solution)/shard_map/ppermute | solution.py:214
  51.4 2.3 %all-to-all-done = bf16[8,64,512]{2,1,0:T(8,128)(2,1)S(1)} async-done(((bf16[8,64,512]{2,1,0:T(8,128)(2,1)}), bf16[8,64,512]{2,1,0:T(8,128)(2,1)S(1)}, u32[]{:S(2)}, u32[]{:S(2)}) %all-to-all-start) | async-done | bytes 524320 | tf_op jit(solution)/shard_map/all_to_all | solution.py:194
  53.9 5.5 %all_to_all.35.x_ref = bf16[2,8,64,512]{3,2,1,0:T(8,128)(2,1)} all-to-all(bf16[2,8,64,512]{3,2,1,0:T(8,128)(2,1)S(1)} %broadcast_in_dim.13), channel_id=1, replica_groups=mesh['y'=4,'zh'=2,'x'=4,'zl'=8,'co'=2] {'co'}, dimensions={0} | all-to-all | bytes 2097152 | tf_op jit(solution)/shard_map/all_to_all | solution.py:194
  59.4 6.9 %all-to-all-start.3 = ((bf16[16,64,512]{2,1,0:T(8,128)(2,1)}), bf16[16,64,512]{2,1,0:T(8,128)(2,1)S(1)}, u32[]{:S(2)}, u32[]{:S(2)}) async-start(bf16[16,64,512]{2,1,0:T(8,128)(2,1)} %bitcast.14), calls=%async_computation.4 | async-start | bytes 2097152 | tf_op jit(solution)/shard_map/all_to_all | solution.py:194
  66.3 2.9 %backward_plane.1 = f32[2,8,64,512]{3,2,1,0:T(8,128)} custom-call(bf16[864,1024]{1,0:T(8,128)(2,1)S(1)} %bitcast.32, bf16[3,32,512]{2,1,0:T(8,128)(2,1)S(1)} %pad_maximum_fusion.u_ref), custom_call_target="tpu_custom_call" | custom-call | tf_op jit(solution)/shard_map/backward_plane/pallas_call | solution.py:87
  69.2 13.1 %all-to-all-done.3.a_ref = bf16[16,64,512]{2,1,0:T(8,128)(2,1)S(1)} async-done(((bf16[16,64,512]{2,1,0:T(8,128)(2,1)}), bf16[16,64,512]{2,1,0:T(8,128)(2,1)S(1)}, u32[]{:S(2)}, u32[]{:S(2)}) %all-to-all-start.3) | async-done | bytes 1048608 | tf_op jit(solution)/shard_map/all_to_all | solution.py:194
  82.2 4.8 %all-to-all-start.2 = ((f32[2,8,64,512]{3,2,1,0:T(8,128)}), f32[2,8,64,512]{3,2,1,0:T(8,128)}, u32[]{:S(2)}, u32[]{:S(2)}) async-start(f32[2,8,64,512]{3,2,1,0:T(8,128)} %backward_plane.1), calls=%async_computation.2 | async-start | bytes 4194304 | tf_op jit(solution)/shard_map/all_to_all | solution.py:194
  87.1 24.9 %all-gather.3.cloned.1.call-done = bf16[32,32,512]{2,1,0:T(8,128)(2,1)} async-done(((bf16[2,32,512]{2,1,0:T(8,128)(2,1)}), bf16[32,32,512]{2,1,0:T(8,128)(2,1)}) %all-gather.3.cloned.1.call-update) | async-done | bytes 1048592 | tf_op jit(solution)/shard_map/all_gather | solution.py:218
  113.2 3.2 %filter_planes.1 = f32[2,27,8,128]{3,2,1,0:T(8,128)} custom-call(bf16[16,64,512]{2,1,0:T(8,128)(2,1)S(1)} %all-to-all-done.3.a_ref, bf16[16,2,32,512]{3,2,1,0:T(8,128)(2,1)S(1)} %bitcast.34), custom_call_target="tpu_custom_call" | custom-call | tf_op jit(solution)/shard_map/filter_planes/pallas_call | solution.py:149
  116.4 12.2 %all-to-all-start.4 = ((f32[2,27,8,128]{3,2,1,0:T(8,128)}), f32[2,27,8,128]{3,2,1,0:T(8,128)S(1)}, u32[]{:S(2)}, u32[]{:S(2)}) async-start(f32[2,27,8,128]{3,2,1,0:T(8,128)} %filter_planes.1), calls=%async_computation.5 | async-start | bytes 442368 | tf_op jit(solution)/shard_map/all_to_all | solution.py:194
  128.6 2.9 %reduce_sum.18 = f32[8,64,512]{2,1,0:T(8,128)} reduce(f32[2,8,64,512]{3,2,1,0:T(8,128)} %all-to-all-done.2, f32[]{:T(128)} %constant.2.clone.1), dimensions={0}, to_apply=%region_0.1 | reduce | flops 262144 | bytes 3145732 | tf_op jit(solution)/shard_map/reduce_sum | solution.py:223
  131.5 10.8 %all-to-all-done.4 = f32[2,27,8,128]{3,2,1,0:T(8,128)S(1)} async-done(((f32[2,27,8,128]{3,2,1,0:T(8,128)}), f32[2,27,8,128]{3,2,1,0:T(8,128)S(1)}, u32[]{:S(2)}, u32[]{:S(2)}) %all-to-all-start.4) | async-done | bytes 221216 | tf_op jit(solution)/shard_map/all_to_all | solution.py:194
  142.3 16.6 %all_to_all.36 = bf16[2,27,8,128]{3,2,1,0:T(8,128)(2,1)S(1)} all-to-all(bf16[2,27,8,128]{3,2,1,0:T(8,128)(2,1)S(1)} %broadcast_in_dim.14), channel_id=1, replica_groups=mesh['y'=4,'zh'=2,'x'=4,'zl'=8,'co'=2] {'zh'}, dimensions={0} | all-to-all | bytes 221184 | tf_op jit(solution)/shard_map/all_to_all | solution.py:194
  160.4 5.7 %all-to-all-start.6 = ((bf16[16,2,27,8,128]{4,3,2,1,0:T(8,128)(2,1)}), bf16[16,2,27,8,128]{4,3,2,1,0:T(8,128)(2,1)S(1)}, u32[]{:S(2)}, u32[]{:S(2)}) async-start(bf16[16,2,27,8,128]{4,3,2,1,0:T(8,128)(2,1)} %broadcast_in_dim.15), calls=%async_computation.7 | async-start | bytes 3538944 | tf_op jit(solution)/shard_map/all_to_all | solution.py:194
  166.1 2.4 %forward_plane.1 = f32[3,32,512]{2,1,0:T(8,128)S(1)} custom-call(bf16[864,1024]{1,0:T(8,128)(2,1)S(1)} %bitcast.33, bf16[2,8,64,512]{3,2,1,0:T(8,128)(2,1)} %all_to_all.35.x_ref), custom_call_target="tpu_custom_call" | custom-call | tf_op jit(solution)/shard_map/forward_plane/pallas_call | solution.py:58
  168.5 3.4 %collective-permute-start.1 = (f32[32,512]{1,0:T(8,128)S(1)}, f32[32,512]{1,0:T(8,128)S(1)}, u32[]{:S(2)}, u32[]{:S(2)}) collective-permute-start(f32[32,512]{1,0:T(8,128)S(1)} %get-tuple-element.4), channel_id=1, source_target_pairs={{0,16},{16,32},{32,48},{48,64},{64,80},{80,96},{96,112},{112,128},... | collective-permute-start | bytes 196616 | tf_op jit(solution)/shard_map/ppermute | solution.py:232
  171.9 14.2 %collective-permute-start = (f32[32,512]{1,0:T(8,128)S(1)}, f32[32,512]{1,0:T(8,128)S(1)}, u32[]{:S(2)}, u32[]{:S(2)}) collective-permute-start(f32[32,512]{1,0:T(8,128)S(1)} %get-tuple-element.3), channel_id=1, source_target_pairs={{16,0},{32,16},{48,32},{64,48},{80,64},{96,80},{112,96},{128,112},... | collective-permute-start | bytes 196616 | tf_op jit(solution)/shard_map/ppermute | solution.py:231
  186.1 1.9 collective-permute-done.1
  188.0 1.9 collective-permute-done
  190.5 12.4 %reduce-scatter.2.cloned.1.call-done = f32[64,512]{1,0:T(8,128)} async-done(((f32[512,512]{1,0:T(8,128)}), f32[64,512]{1,0:T(8,128)}) %reduce-scatter.2.cloned.1.call-update) | async-done | bytes 131088 | tf_op jit(solution)/shard_map/reduce_scatter | solution.py:224
  205.7 6.4 %join_pieces.1 = bf16[27,32,1024]{2,1,0:T(8,128)(2,1)} custom-call(bf16[16,2,27,8,128]{4,3,2,1,0:T(8,128)(2,1)} %copy-done.2), custom_call_target="tpu_custom_call" | custom-call | tf_op jit(solution)/shard_map/join_pieces/pallas_call | solution.py:183
  (27 shorter events, 8.6 us)
Async XLA Ops:
  8.0 42.8 %copy-start.3 = (bf16[32,1,512]{2,0,1:T(8,128)(2,1)S(1)}, bf16[32,1,512]{2,0,1:T(8,128)(2,1)}, u32[]{:S(2)}) copy-start(bf16[32,1,512]{2,0,1:T(8,128)(2,1)} %param.4) | copy-start | bytes 98308
  9.7 44.1 %all-to-all-start = ((bf16[8,64,512]{2,1,0:T(8,128)(2,1)}), bf16[8,64,512]{2,1,0:T(8,128)(2,1)S(1)}, u32[]{:S(2)}, u32[]{:S(2)}) async-start(bf16[8,64,512]{2,1,0:T(8,128)(2,1)} %broadcast_in_dim.12), calls=%async_computation | async-start | bytes 1048576 | tf_op jit(solution)/shard_map/all_to_all | solution.py:194
  22.2 89.8 %all-gather.3.cloned.1.call-start = ((), (), s32[]{:S(2)}) async-start(), calls=%async_computation.9 | async-start | bytes 1114112 | tf_op jit(solution)/shard_map/all_gather | solution.py:218
  22.3 12.5 %collective-permute-start.3 = (bf16[32,512]{1,0:T(8,128)(2,1)}, bf16[32,512]{1,0:T(8,128)(2,1)S(1)}, u32[]{:S(2)}, u32[]{:S(2)}) collective-permute-start(bf16[32,512]{1,0:T(8,128)(2,1)} %bitcast.39), channel_id=1, source_target_pairs={{16,0},{32,16},{48,32},{64,48},{80,64},{96,80},{112,96},{128,112},... | collective-permute-start | bytes 98312 | tf_op jit(solution)/shard_map/ppermute | solution.py:215
  32.9 17.9 %collective-permute-start.2 = (bf16[32,512]{1,0:T(8,128)(2,1)}, bf16[32,512]{1,0:T(8,128)(2,1)S(1)}, u32[]{:S(2)}, u32[]{:S(2)}) collective-permute-start(bf16[32,512]{1,0:T(8,128)(2,1)} %bitcast.40), channel_id=1, source_target_pairs={{0,16},{16,32},{32,48},{48,64},{64,80},{80,96},{96,112},{112,128},... | collective-permute-start | bytes 98312 | tf_op jit(solution)/shard_map/ppermute | solution.py:214
  53.9 12.4 %copy-start = (bf16[32,27,1024]{2,0,1:T(8,128)(2,1)S(1)}, bf16[32,27,1024]{2,0,1:T(8,128)(2,1)}, u32[]{:S(2)}) copy-start(bf16[32,27,1024]{2,0,1:T(8,128)(2,1)} %param.5) | copy-start | bytes 5308420
  59.4 22.9 %all-to-all-start.3 = ((bf16[16,64,512]{2,1,0:T(8,128)(2,1)}), bf16[16,64,512]{2,1,0:T(8,128)(2,1)S(1)}, u32[]{:S(2)}, u32[]{:S(2)}) async-start(bf16[16,64,512]{2,1,0:T(8,128)(2,1)} %bitcast.14), calls=%async_computation.4 | async-start | bytes 2097152 | tf_op jit(solution)/shard_map/all_to_all | solution.py:194
  82.2 34.2 %all-to-all-start.2 = ((f32[2,8,64,512]{3,2,1,0:T(8,128)}), f32[2,8,64,512]{3,2,1,0:T(8,128)}, u32[]{:S(2)}, u32[]{:S(2)}) async-start(f32[2,8,64,512]{3,2,1,0:T(8,128)} %backward_plane.1), calls=%async_computation.2 | async-start | bytes 4194304 | tf_op jit(solution)/shard_map/all_to_all | solution.py:194
  112.0 1.2 copy-start.1
  116.4 25.8 %all-to-all-start.4 = ((f32[2,27,8,128]{3,2,1,0:T(8,128)}), f32[2,27,8,128]{3,2,1,0:T(8,128)S(1)}, u32[]{:S(2)}, u32[]{:S(2)}) async-start(f32[2,27,8,128]{3,2,1,0:T(8,128)} %filter_planes.1), calls=%async_computation.5 | async-start | bytes 442368 | tf_op jit(solution)/shard_map/all_to_all | solution.py:194
  128.6 74.4 %reduce-scatter.2.cloned.1.call-start = ((), (), s32[]{:S(2)}) async-start(), calls=%async_computation.8 | async-start | bytes 1179648 | tf_op jit(solution)/shard_map/reduce_scatter | solution.py:224
  160.4 44.1 %all-to-all-start.6 = ((bf16[16,2,27,8,128]{4,3,2,1,0:T(8,128)(2,1)}), bf16[16,2,27,8,128]{4,3,2,1,0:T(8,128)(2,1)S(1)}, u32[]{:S(2)}, u32[]{:S(2)}) async-start(bf16[16,2,27,8,128]{4,3,2,1,0:T(8,128)(2,1)} %broadcast_in_dim.15), calls=%async_computation.7 | async-start | bytes 3538944 | tf_op jit(solution)/shard_map/all_to_all | solution.py:194
  168.5 19.4 %collective-permute-start.1 = (f32[32,512]{1,0:T(8,128)S(1)}, f32[32,512]{1,0:T(8,128)S(1)}, u32[]{:S(2)}, u32[]{:S(2)}) collective-permute-start(f32[32,512]{1,0:T(8,128)S(1)} %get-tuple-element.4), channel_id=1, source_target_pairs={{0,16},{16,32},{32,48},{48,64},{64,80},{80,96},{96,112},{112,128},... | collective-permute-start | bytes 196616 | tf_op jit(solution)/shard_map/ppermute | solution.py:232
  171.9 18.0 %collective-permute-start = (f32[32,512]{1,0:T(8,128)S(1)}, f32[32,512]{1,0:T(8,128)S(1)}, u32[]{:S(2)}, u32[]{:S(2)}) collective-permute-start(f32[32,512]{1,0:T(8,128)S(1)} %get-tuple-element.3), channel_id=1, source_target_pairs={{16,0},{32,16},{48,32},{64,48},{80,64},{96,80},{112,96},{128,112},... | collective-permute-start | bytes 196616 | tf_op jit(solution)/shard_map/ppermute | solution.py:231
  204.5 1.2 copy-start.2
Sparse Core Ops, SparseCore 0:
  51.6 60.3 all-gather.2
Sparse Core Ops, SparseCore 1:
  131.9 71.0 reduce-scatter.1

commit v2 on v1

--- a/solution.py
+++ b/solution.py
@@ -72,43 +72,36 @@
             for c in range(3):
                 k = 9 * a + 3 * b + c
                 cols[rows * k : rows * (k + 1), :] = moved(plane, 1 - b, 1 - c).astype(BF16)
-    ch = o_ref.shape[2]
-    cores = o_ref.shape[0]
-    for z in range(o_ref.shape[1]):
-        part = w_ref[:, ch * cores * z : ch * cores * (z + 1)]
-        got = lax.dot_general(part, cols[...], (((0,), (0,)), ((), ())), preferred_element_type=F32)
-        for e in range(cores):
-            o_ref[e, z] = got[ch * e : ch * (e + 1)]
-
-
-def backward(w_rows, planes, cores, chips):
+    ch = o_ref.shape[1]
+    for t in range(o_ref.shape[0]):
+        part = w_ref[:, ch * t : ch * (t + 1)]
+        o_ref[t] = lax.dot_general(part, cols[...], (((0,), (0,)), ((), ())), preferred_element_type=F32)
+
+
+def backward(w_rows, planes):
     width = w_rows.shape[1]
     rows = planes.shape[1]
     return pl.pallas_call(
         backward_kernel,
-        out_shape=jax.ShapeDtypeStruct((cores, chips, width // (cores * chips), PLANE), F32),
+        out_shape=jax.ShapeDtypeStruct((width // 128, 128, PLANE), F32),
         scratch_shapes=[pltpu.VMEM((27 * rows, PLANE), BF16)],
         compiler_params=pltpu.CompilerParams(vmem_limit_bytes=32 * 2**20),
         name="backward_plane",
     )(w_rows, planes)
 
 
-def filter_kernel(a_ref, u_ref, o_ref, lhs, rhs, acc):
+def filter_kernel(own_ref, a_ref, u_ref, o_ref, lhs, rhs, acc):
     run, chans = a_ref.shape[0], a_ref.shape[1]
-    rows = u_ref.shape[2]
+    rows = u_ref.shape[3]
 
     @pl.when(pl.program_id(0) == 0)
     def _():
         acc[...] = jnp.zeros_like(acc)
 
     for q in range(run + 2):
-        if q == 0:
-            plane = u_ref[0, 1]
-        elif q == run + 1:
-            plane = u_ref[run - 1, 1]
-        else:
-            plane = u_ref[q - 1, 0]
-        plane = plane.astype(F32)
+        holder = min(max(q - 1, 0), run - 1)
+        entry = lax.rem(own_ref[1] - holder + run, run)
+        plane = u_ref[0, entry, 0 if holder == q - 1 else 1].astype(F32)
         for c in range(3):
             lhs[q, rows * c : rows * (c + 1), :] = moved(plane, 0, 1 - c).astype(BF16)
     for q in range(run):
@@ -142,27 +135,30 @@
                     o_ref[h, k] = jnp.where(low, one, two)
 
 
-def filter_grad(acts, ups, runs):
-    planes, chans = acts.shape[0], acts.shape[1]
-    rows = ups.shape[2]
-    run = planes // runs
-    return pl.pallas_call(
-        filter_kernel,
+def filter_grad(acts, ups, own):
+    chans = acts.shape[1]
+    runs, run, _, rows = ups.shape[:4]
+    spec = pltpu.PrefetchScalarGridSpec(
+        num_scalar_prefetch=1,
         grid=(runs,),
         in_specs=[
-            pl.BlockSpec((run, chans, PLANE), lambda r: (r, 0, 0)),
-            pl.BlockSpec((run, 2, rows, PLANE), lambda r: (r, 0, 0, 0)),
+            pl.BlockSpec((run, chans, PLANE), lambda r, own: (r, 0, 0)),
+            pl.BlockSpec((1, run, 2, rows, PLANE), lambda r, own: (lax.rem(own[0] - r + runs, runs), 0, 0, 0, 0)),
         ],
-        out_specs=pl.BlockSpec((rows // 16, 27, 8, 128), lambda r: (0, 0, 0, 0)),
-        out_shape=jax.ShapeDtypeStruct((rows // 16, 27, 8, 128), F32),
+        out_specs=pl.BlockSpec((rows // 16, 27, 8, 128), lambda r, own: (0, 0, 0, 0)),
         scratch_shapes=[
             pltpu.VMEM((run + 2, 3 * rows, PLANE), BF16),
             pltpu.VMEM((run, 3 * chans, PLANE), BF16),
             pltpu.VMEM((9 * rows, 3 * chans), F32),
         ],
+    )
+    return pl.pallas_call(
+        filter_kernel,
+        grid_spec=spec,
+        out_shape=jax.ShapeDtypeStruct((rows // 16, 27, 8, 128), F32),
         compiler_params=pltpu.CompilerParams(vmem_limit_bytes=32 * 2**20),
         name="filter_planes",
-    )(acts, ups)
+    )(own, acts, ups)
 
 
 def join_kernel(r_ref, o_ref, *, order):
@@ -198,6 +194,14 @@
     return exchange(jnp.broadcast_to(value, (lax.axis_size(axes), *value.shape)), axes)
 
 
+def from_before(value, axis):
+    size = lax.axis_size(axis)
+    pieces = [value]
+    for d in range(1, size):
+        pieces.append(lax.ppermute(value, axis, [(i, (i + d) % size) for i in range(size)]))
+    return pieces
+
+
 def local(activations, upstream, weights):
     ch, co = activations.shape[0], upstream.shape[0]
     n_vox, n_x, n_y = lax.axis_size(VOX), lax.axis_size("x"), lax.axis_size("y")
@@ -215,24 +219,23 @@
     after = lax.ppermute(ups, VOX, down)
     edge = jnp.where(lax.axis_index("x") == 0, before, after)
     up_planes = jnp.stack([ups, edge])
-    up_planes = lax.all_gather(up_planes, XY, axis=0, tiled=False)
+    row = jnp.stack(from_before(up_planes, "x"))
+    up_planes = jnp.stack(from_before(row, "y"))
 
     w_rows = weights.transpose(1, 0, 2).reshape(27 * co, cin)
-    part = backward(w_rows, jnp.stack([before, ups, after]), n_co, n_zl)
-    part = exchange(part, "co")
-    part = jnp.sum(part, axis=0)
-    part = lax.psum_scatter(part.reshape(n_zl * ch, PLANE), "zl", scatter_dimension=0, tiled=True)
+    part = backward(w_rows, jnp.stack([before, ups, after]))
+    part = lax.psum_scatter(part.reshape(cin, PLANE), CHAN, scatter_dimension=0, tiled=True)
     input_grad = part.astype(BF16).reshape(ch, 1, PLANE)
 
     plane = shared(near, "co")
 
     acts = exchange(plane.reshape(n_xy, ch, PLANE), XY)
     around = forward(w_rows, plane)
-    from_after = lax.ppermute(around[2], VOX, down)
-    from_before = lax.ppermute(around[0], VOX, up)
-    outputs = (around[1] + from_after + from_before).astype(BF16).reshape(co, 1, PLANE)
-
-    raw = filter_grad(acts, up_planes, n_y)
+    after_part = lax.ppermute(around[2], VOX, down)
+    before_part = lax.ppermute(around[0], VOX, up)
+    outputs = (around[1] + after_part + before_part).astype(BF16).reshape(co, 1, PLANE)
+
+    raw = filter_grad(acts, up_planes, jnp.stack([lax.axis_index("y"), lax.axis_index("x")]))
     raw = exchange(raw, "zh")
     raw = jnp.sum(raw, axis=0)
     scale = 1.0 / jnp.sqrt(jnp.float32(n_vox * PLANE))

time: 221 us -> 204 us (0.923)
  the two profiles are of different devices: /device:TPU:24 before, /device:TPU:454 now
where the time goes in v2:
time: 204 us; the launch traced here: 203 us
  starting transfers between devices  80.8 us (40%)
  blocking collectives  45.2 us (22%)
  waiting for transfers between devices  37 us (18%)
  Pallas kernels  14.8 us (7%)
  between operations  14.2 us (7%)
  local copies, waits for them, and re-layouts  5.85 us (3%)
  other arithmetic  5.32 us (3%)
    all_to_all x3, blocking collectives, exchange(): return lax.all_to_all(pieces, axes, 0, 0, tiled=True)  45.2 us
    all_to_all x3, starting transfers between devices, exchange(): return lax.all_to_all(pieces, axes, 0, 0, tiled=True)  27.8 us
    ppermute x6, starting transfers between devices, from_before(): lax.ppermute(value, axis, [(i, (i + d) % size) for i in range(size)])  19.9 us
    ppermute x6, waiting for transfers between devices, from_before(): lax.ppermute(value, axis, [(i, (i + d) % size) for i in range(size)])  16.5 us
    ppermute x1, waiting for transfers between devices, local(): after_part = lax.ppermute(around[2], VOX, down)  15.2 us
    ppermute x1, starting transfers between devices, local(): before = lax.ppermute(ups, VOX, up)  14.8 us
    ppermute x1, starting transfers between devices, local(): before_part = lax.ppermute(around[0], VOX, up)  13.6 us
    pallas_call x1, Pallas kernels, join(): pl.pallas_call(functools.partial(join_kernel, order=order), grid=(9,), in...  6.43 us
  transfers between devices with their start and end apart: 14, of which 9 were waited for; matrix products, arithmetic and copies ran while one was open for 3% of the time, Pallas kernels for 4%

profile of v2, /device:TPU:454, one launch (start us, length us, event | category | flops | bytes accessed | tf_op | source)
XLA Modules:
  0.0 203.2 jit_solution(15033623486502213863)
XLA Ops:
  9.0 9.5 %all-to-all-start = ((bf16[8,64,512]{2,1,0:T(8,128)(2,1)}), bf16[8,64,512]{2,1,0:T(8,128)(2,1)S(1)}, u32[]{:S(2)}, u32[]{:S(2)}) async-start(bf16[8,64,512]{2,1,0:T(8,128)(2,1)} %broadcast_in_dim.12), calls=%async_computation | async-start | bytes 1048576 | tf_op jit(solution)/shard_map/all_to_all | solution.py:190
  18.4 2.7 %collective-permute-start.3 = (bf16[32,512]{1,0:T(8,128)(2,1)}, bf16[32,512]{1,0:T(8,128)(2,1)S(1)}, u32[]{:S(2)}, u32[]{:S(2)}) collective-permute-start(bf16[32,512]{1,0:T(8,128)(2,1)} %bitcast.48), channel_id=1, source_target_pairs={{16,0},{32,16},{48,32},{64,48},{80,64},{96,80},{112,96},{128,112},... | collective-permute-start | bytes 98312 | tf_op jit(solution)/shard_map/ppermute | solution.py:219
  21.2 14.8 %collective-permute-start.2 = (bf16[32,512]{1,0:T(8,128)(2,1)}, bf16[32,512]{1,0:T(8,128)(2,1)S(1)}, u32[]{:S(2)}, u32[]{:S(2)}) collective-permute-start(bf16[32,512]{1,0:T(8,128)(2,1)} %bitcast.49), channel_id=1, source_target_pairs={{0,16},{16,32},{32,48},{48,64},{64,80},{80,96},{96,112},{112,128},... | collective-permute-start | bytes 98312 | tf_op jit(solution)/shard_map/ppermute | solution.py:218
  39.7 2.9 %backward_plane.1 = f32[8,128,512]{2,1,0:T(8,128)} custom-call(bf16[864,1024]{1,0:T(8,128)(2,1)S(1)} %bitcast.43, bf16[3,32,512]{2,1,0:T(8,128)(2,1)S(1)} %pad_maximum_fusion.2.u_ref), custom_call_target="tpu_custom_call" | custom-call | tf_op jit(solution)/shard_map/backward_plane/pallas_call | solution.py:84
  42.7 5.4 %all_to_all.30.x_ref = bf16[2,8,64,512]{3,2,1,0:T(8,128)(2,1)} all-to-all(bf16[2,8,64,512]{3,2,1,0:T(8,128)(2,1)S(1)} %broadcast_in_dim.13), channel_id=1, replica_groups=mesh['y'=4,'zh'=2,'x'=4,'zl'=8,'co'=2] {'co'}, dimensions={0} | all-to-all | bytes 2097152 | tf_op jit(solution)/shard_map/all_to_all | solution.py:190
  48.1 11.6 %all-to-all-start.2 = ((bf16[16,64,512]{2,1,0:T(8,128)(2,1)}), bf16[16,64,512]{2,1,0:T(8,128)(2,1)S(1)}, u32[]{:S(2)}, u32[]{:S(2)}) async-start(bf16[16,64,512]{2,1,0:T(8,128)(2,1)} %bitcast.16), calls=%async_computation.3 | async-start | bytes 2097152 | tf_op jit(solution)/shard_map/all_to_all | solution.py:190
  59.7 2.8 %collective-permute-start.6 = (bf16[2,32,512]{2,1,0:T(8,128)(2,1)S(1)}, bf16[2,32,512]{2,1,0:T(8,128)(2,1)S(1)}, u32[]{:S(2)}, u32[]{:S(2)}) collective-permute-start(bf16[2,32,512]{2,1,0:T(8,128)(2,1)S(1)} %get-tuple-element.8), channel_id=1, source_target_pairs={{0,48},{16,0},{32,16},{48,32},{1,49},{17,1},{33,17},{49,33},{2,50}... | collective-permute-start | bytes 196616 | tf_op jit(solution)/shard_map/ppermute | solution.py:201
  62.5 2.6 %collective-permute-start.5 = (bf16[2,32,512]{2,1,0:T(8,128)(2,1)S(1)}, bf16[2,32,512]{2,1,0:T(8,128)(2,1)S(1)}, u32[]{:S(2)}, u32[]{:S(2)}) collective-permute-start(bf16[2,32,512]{2,1,0:T(8,128)(2,1)S(1)} %get-tuple-element.8), channel_id=1, source_target_pairs={{0,32},{16,48},{32,0},{48,16},{1,33},{17,49},{33,1},{49,17},{2,34}... | collective-permute-start | bytes 196616 | tf_op jit(solution)/shard_map/ppermute | solution.py:201
  65.1 4.4 %collective-permute-start.4 = (bf16[2,32,512]{2,1,0:T(8,128)(2,1)S(1)}, bf16[2,32,512]{2,1,0:T(8,128)(2,1)S(1)}, u32[]{:S(2)}, u32[]{:S(2)}) collective-permute-start(bf16[2,32,512]{2,1,0:T(8,128)(2,1)S(1)} %get-tuple-element.8), channel_id=1, source_target_pairs={{0,16},{16,32},{32,48},{48,0},{1,17},{17,33},{33,49},{49,1},{2,18}... | collective-permute-start | bytes 196616 | tf_op jit(solution)/shard_map/ppermute | solution.py:201
  69.5 3.7 %collective-permute-done.6 = bf16[2,32,512]{2,1,0:T(8,128)(2,1)S(1)} collective-permute-done((bf16[2,32,512]{2,1,0:T(8,128)(2,1)S(1)}, bf16[2,32,512]{2,1,0:T(8,128)(2,1)S(1)}, u32[]{:S(2)}, u32[]{:S(2)}) %collective-permute-start.6) | collective-permute-done | bytes 65568 | tf_op jit(solution)/shard_map/ppermute | solution.py:201
  73.2 2.6 %collective-permute-done.5 = bf16[2,32,512]{2,1,0:T(8,128)(2,1)S(1)} collective-permute-done((bf16[2,32,512]{2,1,0:T(8,128)(2,1)S(1)}, bf16[2,32,512]{2,1,0:T(8,128)(2,1)S(1)}, u32[]{:S(2)}, u32[]{:S(2)}) %collective-permute-start.5) | collective-permute-done | bytes 65568 | tf_op jit(solution)/shard_map/ppermute | solution.py:201
  75.9 4.6 %collective-permute-start.9 = (bf16[4,2,32,512]{3,2,1,0:T(8,128)(2,1)S(1)}, bf16[4,2,32,512]{3,2,1,0:T(8,128)(2,1)}, u32[]{:S(2)}, u32[]{:S(2)}) collective-permute-start(bf16[4,2,32,512]{3,2,1,0:T(8,128)(2,1)S(1)} %get-tuple-element.4), channel_id=1, source_target_pairs={{0,384},{128,0},{256,128},{384,256},{1,385},{129,1},{257,129},{385... | collective-permute-start | bytes 786440 | tf_op jit(solution)/shard_map/ppermute | solution.py:201
  80.5 2.8 %collective-permute-start.8 = (bf16[4,2,32,512]{3,2,1,0:T(8,128)(2,1)S(1)}, bf16[4,2,32,512]{3,2,1,0:T(8,128)(2,1)}, u32[]{:S(2)}, u32[]{:S(2)}) collective-permute-start(bf16[4,2,32,512]{3,2,1,0:T(8,128)(2,1)S(1)} %get-tuple-element.4), channel_id=1, source_target_pairs={{0,256},{128,384},{256,0},{384,128},{1,257},{129,385},{257,1},{385... | collective-permute-start | bytes 786440 | tf_op jit(solution)/shard_map/ppermute | solution.py:201
  83.3 2.8 %collective-permute-start.7 = (bf16[4,2,32,512]{3,2,1,0:T(8,128)(2,1)S(1)}, bf16[4,2,32,512]{3,2,1,0:T(8,128)(2,1)}, u32[]{:S(2)}, u32[]{:S(2)}) collective-permute-start(bf16[4,2,32,512]{3,2,1,0:T(8,128)(2,1)S(1)} %get-tuple-element.4), channel_id=1, source_target_pairs={{0,128},{128,256},{256,384},{384,0},{1,129},{129,257},{257,385},{3... | collective-permute-start | bytes 786440 | tf_op jit(solution)/shard_map/ppermute | solution.py:201
  86.1 4.5 %collective-permute-done.9 = bf16[4,2,32,512]{3,2,1,0:T(8,128)(2,1)} collective-permute-done((bf16[4,2,32,512]{3,2,1,0:T(8,128)(2,1)S(1)}, bf16[4,2,32,512]{3,2,1,0:T(8,128)(2,1)}, u32[]{:S(2)}, u32[]{:S(2)}) %collective-permute-start.9) | collective-permute-done | bytes 262176 | tf_op jit(solution)/shard_map/ppermute | solution.py:201
  90.6 2.6 %collective-permute-done.8 = bf16[4,2,32,512]{3,2,1,0:T(8,128)(2,1)} collective-permute-done((bf16[4,2,32,512]{3,2,1,0:T(8,128)(2,1)S(1)}, bf16[4,2,32,512]{3,2,1,0:T(8,128)(2,1)}, u32[]{:S(2)}, u32[]{:S(2)}) %collective-permute-start.8) | collective-permute-done | bytes 262176 | tf_op jit(solution)/shard_map/ppermute | solution.py:201
  93.2 3.1 %collective-permute-done.7 = bf16[4,2,32,512]{3,2,1,0:T(8,128)(2,1)} collective-permute-done((bf16[4,2,32,512]{3,2,1,0:T(8,128)(2,1)S(1)}, bf16[4,2,32,512]{3,2,1,0:T(8,128)(2,1)}, u32[]{:S(2)}, u32[]{:S(2)}) %collective-permute-start.7) | collective-permute-done | bytes 262176 | tf_op jit(solution)/shard_map/ppermute | solution.py:201
  99.7 3.1 %filter_planes.1 = f32[2,27,8,128]{3,2,1,0:T(8,128)S(1)} custom-call(s32[2]{0:T(128)S(1)} %pad_add_fusion.own_ref, bf16[16,64,512]{2,1,0:T(8,128)(2,1)S(1)} %all-to-all-done.2.a_ref, bf16[4,4,2,32,512]{4,3,2,1,0:T(8,128)(2,1)S(1)} %copy-done.1), custom_call_target="tpu_custom_call" | custom-call | tf_op jit(solution)/shard_map/filter_planes/pallas_call | solution.py:155
  102.8 22.8 %all_to_all.31 = f32[2,27,8,128]{3,2,1,0:T(8,128)S(1)} all-to-all(f32[2,27,8,128]{3,2,1,0:T(8,128)S(1)} %filter_planes.1), channel_id=1, replica_groups=mesh['y'=4,'zh'=2,'x'=4,'zl'=8,'co'=2] {'zh'}, dimensions={0} | all-to-all | bytes 442368 | tf_op jit(solution)/shard_map/all_to_all | solution.py:190
  125.6 17.1 %all_to_all.32 = bf16[2,27,8,128]{3,2,1,0:T(8,128)(2,1)S(1)} all-to-all(bf16[2,27,8,128]{3,2,1,0:T(8,128)(2,1)S(1)} %broadcast_in_dim.14), channel_id=1, replica_groups=mesh['y'=4,'zh'=2,'x'=4,'zl'=8,'co'=2] {'zh'}, dimensions={0} | all-to-all | bytes 221184 | tf_op jit(solution)/shard_map/all_to_all | solution.py:190
  144.1 6.7 %all-to-all-start.5 = ((bf16[16,2,27,8,128]{4,3,2,1,0:T(8,128)(2,1)}), bf16[16,2,27,8,128]{4,3,2,1,0:T(8,128)(2,1)S(1)}, u32[]{:S(2)}, u32[]{:S(2)}) async-start(bf16[16,2,27,8,128]{4,3,2,1,0:T(8,128)(2,1)} %broadcast_in_dim.15), calls=%async_computation.6 | async-start | bytes 3538944 | tf_op jit(solution)/shard_map/all_to_all | solution.py:190
  153.3 13.6 %collective-permute-start.1 = (f32[32,512]{1,0:T(8,128)S(1)}, f32[32,512]{1,0:T(8,128)S(1)}, u32[]{:S(2)}, u32[]{:S(2)}) collective-permute-start(f32[32,512]{1,0:T(8,128)S(1)} %get-tuple-element.6), channel_id=1, source_target_pairs={{0,16},{16,32},{32,48},{48,64},{64,80},{80,96},{96,112},{112,128},... | collective-permute-start | bytes 196616 | tf_op jit(solution)/shard_map/ppermute | solution.py:235
  171.2 15.2 %collective-permute-done = f32[32,512]{1,0:T(8,128)S(1)} collective-permute-done((f32[32,512]{1,0:T(8,128)S(1)}, f32[32,512]{1,0:T(8,128)S(1)}, u32[]{:S(2)}, u32[]{:S(2)}) %collective-permute-start) | collective-permute-done | bytes 65568 | tf_op jit(solution)/shard_map/ppermute | solution.py:234
  189.9 6.4 %join_pieces.1 = bf16[27,32,1024]{2,1,0:T(8,128)(2,1)} custom-call(bf16[16,2,27,8,128]{4,3,2,1,0:T(8,128)(2,1)} %copy-done.2), custom_call_target="tpu_custom_call" | custom-call | tf_op jit(solution)/shard_map/join_pieces/pallas_call | solution.py:179
  (35 shorter events, 20.8 us)
Async XLA Ops:
  7.2 32.6 %copy-start = (bf16[32,27,1024]{2,0,1:T(8,128)(2,1)S(1)}, bf16[32,27,1024]{2,0,1:T(8,128)(2,1)}, u32[]{:S(2)}) copy-start(bf16[32,27,1024]{2,0,1:T(8,128)(2,1)} %param.5) | copy-start | bytes 5308420
  9.0 33.6 %all-to-all-start = ((bf16[8,64,512]{2,1,0:T(8,128)(2,1)}), bf16[8,64,512]{2,1,0:T(8,128)(2,1)S(1)}, u32[]{:S(2)}, u32[]{:S(2)}) async-start(bf16[8,64,512]{2,1,0:T(8,128)(2,1)} %broadcast_in_dim.12), calls=%async_computation | async-start | bytes 1048576 | tf_op jit(solution)/shard_map/all_to_all | solution.py:190
  18.4 168.7 %reduce-scatter.2.cloned.1.call-start = ((), (), s32[]{:S(2)}) async-start(), calls=%async_computation.7 | async-start | bytes 2228224 | tf_op jit(solution)/shard_map/reduce_scatter | solution.py:227
  18.4 18.4 %collective-permute-start.3 = (bf16[32,512]{1,0:T(8,128)(2,1)}, bf16[32,512]{1,0:T(8,128)(2,1)S(1)}, u32[]{:S(2)}, u32[]{:S(2)}) collective-permute-start(bf16[32,512]{1,0:T(8,128)(2,1)} %bitcast.48), channel_id=1, source_target_pairs={{16,0},{32,16},{48,32},{64,48},{80,64},{96,80},{112,96},{128,112},... | collective-permute-start | bytes 98312 | tf_op jit(solution)/shard_map/ppermute | solution.py:219
  21.2 17.8 %collective-permute-start.2 = (bf16[32,512]{1,0:T(8,128)(2,1)}, bf16[32,512]{1,0:T(8,128)(2,1)S(1)}, u32[]{:S(2)}, u32[]{:S(2)}) collective-permute-start(bf16[32,512]{1,0:T(8,128)(2,1)} %bitcast.49), channel_id=1, source_target_pairs={{0,16},{16,32},{32,48},{48,64},{64,80},{80,96},{96,112},{112,128},... | collective-permute-start | bytes 98312 | tf_op jit(solution)/shard_map/ppermute | solution.py:218
  42.7 17.0 %copy-start.3 = (bf16[32,1,512]{2,0,1:T(8,128)(2,1)S(1)}, bf16[32,1,512]{2,0,1:T(8,128)(2,1)}, u32[]{:S(2)}) copy-start(bf16[32,1,512]{2,0,1:T(8,128)(2,1)} %param.4) | copy-start | bytes 98308
  48.1 50.4 %all-to-all-start.2 = ((bf16[16,64,512]{2,1,0:T(8,128)(2,1)}), bf16[16,64,512]{2,1,0:T(8,128)(2,1)S(1)}, u32[]{:S(2)}, u32[]{:S(2)}) async-start(bf16[16,64,512]{2,1,0:T(8,128)(2,1)} %bitcast.16), calls=%async_computation.3 | async-start | bytes 2097152 | tf_op jit(solution)/shard_map/all_to_all | solution.py:190
  59.7 13.5 %collective-permute-start.6 = (bf16[2,32,512]{2,1,0:T(8,128)(2,1)S(1)}, bf16[2,32,512]{2,1,0:T(8,128)(2,1)S(1)}, u32[]{:S(2)}, u32[]{:S(2)}) collective-permute-start(bf16[2,32,512]{2,1,0:T(8,128)(2,1)S(1)} %get-tuple-element.8), channel_id=1, source_target_pairs={{0,48},{16,0},{32,16},{48,32},{1,49},{17,1},{33,17},{49,33},{2,50}... | collective-permute-start | bytes 196616 | tf_op jit(solution)/shard_map/ppermute | solution.py:201
  62.5 13.4 %collective-permute-start.5 = (bf16[2,32,512]{2,1,0:T(8,128)(2,1)S(1)}, bf16[2,32,512]{2,1,0:T(8,128)(2,1)S(1)}, u32[]{:S(2)}, u32[]{:S(2)}) collective-permute-start(bf16[2,32,512]{2,1,0:T(8,128)(2,1)S(1)} %get-tuple-element.8), channel_id=1, source_target_pairs={{0,32},{16,48},{32,0},{48,16},{1,33},{17,49},{33,1},{49,17},{2,34}... | collective-permute-start | bytes 196616 | tf_op jit(solution)/shard_map/ppermute | solution.py:201
  65.1 10.7 %collective-permute-start.4 = (bf16[2,32,512]{2,1,0:T(8,128)(2,1)S(1)}, bf16[2,32,512]{2,1,0:T(8,128)(2,1)S(1)}, u32[]{:S(2)}, u32[]{:S(2)}) collective-permute-start(bf16[2,32,512]{2,1,0:T(8,128)(2,1)S(1)} %get-tuple-element.8), channel_id=1, source_target_pairs={{0,16},{16,32},{32,48},{48,0},{1,17},{17,33},{33,49},{49,1},{2,18}... | collective-permute-start | bytes 196616 | tf_op jit(solution)/shard_map/ppermute | solution.py:201
  75.9 14.7 %collective-permute-start.9 = (bf16[4,2,32,512]{3,2,1,0:T(8,128)(2,1)S(1)}, bf16[4,2,32,512]{3,2,1,0:T(8,128)(2,1)}, u32[]{:S(2)}, u32[]{:S(2)}) collective-permute-start(bf16[4,2,32,512]{3,2,1,0:T(8,128)(2,1)S(1)} %get-tuple-element.4), channel_id=1, source_target_pairs={{0,384},{128,0},{256,128},{384,256},{1,385},{129,1},{257,129},{385... | collective-permute-start | bytes 786440 | tf_op jit(solution)/shard_map/ppermute | solution.py:201
  80.5 12.7 %collective-permute-start.8 = (bf16[4,2,32,512]{3,2,1,0:T(8,128)(2,1)S(1)}, bf16[4,2,32,512]{3,2,1,0:T(8,128)(2,1)}, u32[]{:S(2)}, u32[]{:S(2)}) collective-permute-start(bf16[4,2,32,512]{3,2,1,0:T(8,128)(2,1)S(1)} %get-tuple-element.4), channel_id=1, source_target_pairs={{0,256},{128,384},{256,0},{384,128},{1,257},{129,385},{257,1},{385... | collective-permute-start | bytes 786440 | tf_op jit(solution)/shard_map/ppermute | solution.py:201
  83.3 13.0 %collective-permute-start.7 = (bf16[4,2,32,512]{3,2,1,0:T(8,128)(2,1)S(1)}, bf16[4,2,32,512]{3,2,1,0:T(8,128)(2,1)}, u32[]{:S(2)}, u32[]{:S(2)}) collective-permute-start(bf16[4,2,32,512]{3,2,1,0:T(8,128)(2,1)S(1)} %get-tuple-element.4), channel_id=1, source_target_pairs={{0,128},{128,256},{256,384},{384,0},{1,129},{129,257},{257,385},{3... | collective-permute-start | bytes 786440 | tf_op jit(solution)/shard_map/ppermute | solution.py:201
  98.5 1.2 copy-start.1
  144.1 44.5 %all-to-all-start.5 = ((bf16[16,2,27,8,128]{4,3,2,1,0:T(8,128)(2,1)}), bf16[16,2,27,8,128]{4,3,2,1,0:T(8,128)(2,1)S(1)}, u32[]{:S(2)}, u32[]{:S(2)}) async-start(bf16[16,2,27,8,128]{4,3,2,1,0:T(8,128)(2,1)} %broadcast_in_dim.15), calls=%async_computation.6 | async-start | bytes 3538944 | tf_op jit(solution)/shard_map/all_to_all | solution.py:190
  153.3 17.9 %collective-permute-start.1 = (f32[32,512]{1,0:T(8,128)S(1)}, f32[32,512]{1,0:T(8,128)S(1)}, u32[]{:S(2)}, u32[]{:S(2)}) collective-permute-start(f32[32,512]{1,0:T(8,128)S(1)} %get-tuple-element.6), channel_id=1, source_target_pairs={{0,16},{16,32},{32,48},{48,64},{64,80},{80,96},{96,112},{112,128},... | collective-permute-start | bytes 196616 | tf_op jit(solution)/shard_map/ppermute | solution.py:235
  166.9 19.5 %collective-permute-start = (f32[32,512]{1,0:T(8,128)S(1)}, f32[32,512]{1,0:T(8,128)S(1)}, u32[]{:S(2)}, u32[]{:S(2)}) collective-permute-start(f32[32,512]{1,0:T(8,128)S(1)} %get-tuple-element.5), channel_id=1, source_target_pairs={{16,0},{32,16},{48,32},{64,48},{80,64},{96,80},{112,96},{128,112},... | collective-permute-start | bytes 196616 | tf_op jit(solution)/shard_map/ppermute | solution.py:234
  188.6 1.2 copy-start.2
Sparse Core Ops, SparseCore 0:
  42.7 104.4 reduce-scatter.1

commit v3 on v2

v3 whole, which is shorter than its diff:
```python
import jax
import jax.numpy as jnp
from jax import lax
from jax.experimental import pallas as pl
from jax.experimental.pallas import tpu as pltpu
from jax.sharding import Mesh
from jax.sharding import PartitionSpec as P


NY = 32
NZ = 16
PLANE = NY * NZ
VOX = ("y", "zh", "x")
XY = ("y", "x")
CHAN = ("zl", "co")
F32 = jnp.float32
BF16 = jnp.bfloat16


def moved(value, b, c):
    step = NZ * b + c
    if step == 0:
        return value
    out = pltpu.roll(value, (-step) % PLANE, 1)
    lane = lax.broadcasted_iota(jnp.int32, value.shape, 1)
    keep = None
    if b != 0:
        keep = (lane + NZ * b >= 0) & (lane + NZ * b < PLANE)
    if c != 0:
        col = lane % NZ + c
        inside = (col >= 0) & (col < NZ)
        keep = inside if keep is None else keep & inside
    return jnp.where(keep, out, 0.0)


def forward_kernel(w_ref, low_ref, high_ref, o_ref, x_rows):
    rows = o_ref.shape[1]
    cores, chips, ch = low_ref.shape[:3]
    for z in range(chips):
        for e in range(cores):
            for half, ref in enumerate((low_ref, high_ref)):
                first = ((z * cores + e) * 2 + half) * ch
                x_rows[first : first + ch, :] = ref[e, z]
    for a in range(3):
        y = jnp.dot(w_ref[9 * rows * a : 9 * rows * (a + 1), :], x_rows[...], preferred_element_type=F32)
        total = None
        for b in range(3):
            for c in range(3):
                k = 3 * b + c
                term = moved(y[rows * k : rows * (k + 1), :], b - 1, c - 1)
                total = term if total is None else total + term
        o_ref[a] = total


def forward(w_rows, low, high):
    rows = w_rows.shape[0] // 27
    return pl.pallas_call(
        forward_kernel,
        out_shape=jax.ShapeDtypeStruct((3, rows, PLANE), F32),
        scratch_shapes=[pltpu.VMEM((w_rows.shape[1], PLANE), BF16)],
        compiler_params=pltpu.CompilerParams(vmem_limit_bytes=32 * 2**20),
        name="forward_plane",
    )(w_rows, low, high)


def backward_kernel(w_ref, u_ref, o_ref, cols):
    rows = u_ref.shape[1]
    for a in range(3):
        plane = u_ref[2 - a].astype(F32)
        for b in range(3):
            for c in range(3):
                k = 9 * a + 3 * b + c
                cols[rows * k : rows * (k + 1), :] = moved(plane, 1 - b, 1 - c).astype(BF16)
    ch = o_ref.shape[1]
    for t in range(o_ref.shape[0]):
        part = w_ref[:, ch * t : ch * (t + 1)]
        o_ref[t] = lax.dot_general(part, cols[...], (((0,), (0,)), ((), ())), preferred_element_type=F32)


def backward(w_rows, planes):
    width = w_rows.shape[1]
    rows = planes.shape[1]
    return pl.pallas_call(
        backward_kernel,
        out_shape=jax.ShapeDtypeStruct((width // 128, 128, PLANE), F32),
        scratch_shapes=[pltpu.VMEM((27 * rows, PLANE), BF16)],
        compiler_params=pltpu.CompilerParams(vmem_limit_bytes=32 * 2**20),
        name="backward_plane",
    )(w_rows, planes)


def filter_kernel(a_ref, u_ref, o_ref, lhs, rhs, acc):
    cores, run, chans = a_ref.shape[:3]
    rows = (u_ref.shape[1] - chans) // 2

    @pl.when(pl.program_id(0) == 0)
    def _():
        acc[...] = jnp.zeros_like(acc)

    for q in range(run + 2):
        holder = min(max(q - 1, 0), run - 1)
        first = chans if holder == q - 1 else chans + rows
        plane = u_ref[holder, first : first + rows, :].astype(F32)
        for c in range(3):
            lhs[q, rows * c : rows * (c + 1), :] = moved(plane, 0, 1 - c).astype(BF16)
    for q in range(run):
        for e in range(cores):
            plane = a_ref[e, q].astype(F32)
            for b in range(3):
                first = chans * (cores * b + e)
                rhs[q, first : first + chans, :] = moved(plane, b - 1, 0).astype(BF16)
    total = acc[...]
    for q in range(run):
        left = lhs[q : q + 3].reshape(9 * rows, PLANE)
        total = total + lax.dot_general(left, rhs[q], (((1,), (1,)), ((), ())), preferred_element_type=F32)
    acc[...] = total

    @pl.when(pl.program_id(0) == pl.num_programs(0) - 1)
    def _():
        group = lax.broadcasted_iota(jnp.int32, (8, 128), 1) // 32
        for k in range(27):
            a, b, c = k // 9, k // 3 % 3, k % 3
            for h in range(o_ref.shape[0]):
                row = rows * (3 * (2 - a) + c) + 16 * h
                sides = []
                for first in (row, row + 8):
                    if b == 2:
                        side = total[first : first + 8, 128:192]
                        side = jnp.concatenate([side, side], axis=1)
                    else:
                        side = total[first : first + 8, 0:128]
                    sides.append(pltpu.roll(side, 64, 1) if b == 1 else side)
                one, two = sides
                left = jnp.where(group == 0, one, pltpu.roll(two, 32, 1))
                right = jnp.where(group == 2, pltpu.roll(one, 32, 1), pltpu.roll(two, 64, 1))
                o_ref[h, k] = jnp.where(group < 2, left, right)


def filter_grad(acts, mixed, runs):
    cores, planes, chans = acts.shape[:3]
    height = mixed.shape[1]
    rows = (height - chans) // 2
    run = planes // runs
    return pl.pallas_call(
        filter_kernel,
        grid=(runs,),
        in_specs=[
            pl.BlockSpec((cores, run, chans, PLANE), lambda r: (0, r, 0, 0)),
            pl.BlockSpec((run, height, PLANE), lambda r: (r, 0, 0)),
        ],
        out_specs=pl.BlockSpec((rows // 16, 27, 8, 128), lambda r: (0, 0, 0, 0)),
        out_shape=jax.ShapeDtypeStruct((rows // 16, 27, 8, 128), F32),
        scratch_shapes=[
            pltpu.VMEM((run + 2, 3 * rows, PLANE), BF16),
            pltpu.VMEM((run, 3 * cores * chans, PLANE), BF16),
            pltpu.VMEM((9 * rows, 3 * cores * chans), F32),
        ],
        compiler_params=pltpu.CompilerParams(vmem_limit_bytes=32 * 2**20),
        name="filter_planes",
    )(acts, mixed)


def join_kernel(r_ref, o_ref):
    even = lax.broadcasted_iota(jnp.int32, (8, 128), 1) // 32 % 2 == 0
    for k in range(o_ref.shape[0]):
        for t in range(r_ref.shape[0] // 2):
            for h in range(r_ref.shape[1]):
                left = r_ref[2 * t, h, k].astype(F32)
                right = r_ref[2 * t + 1, h, k].astype(F32)
                one = jnp.where(even, left, pltpu.roll(right, 32, 1))
                two = jnp.where(even, pltpu.roll(left, 96, 1), right)
                both = jnp.concatenate([one, two], axis=0).astype(BF16)
                o_ref[k, 16 * h : 16 * (h + 1), 128 * t : 128 * (t + 1)] = both


def join(pieces):
    size, halves = pieces.shape[:2]
    return pl.pallas_call(
        join_kernel,
        grid=(9,),
        in_specs=[pl.BlockSpec((size, halves, 3, 8, 128), lambda g: (0, 0, g, 0, 0))],
        out_specs=pl.BlockSpec((3, 16 * halves, 64 * size), lambda g: (g, 0, 0)),
        out_shape=jax.ShapeDtypeStruct((27, 16 * halves, 64 * size), BF16),
        name="join_pieces",
    )(pieces)


def exchange(pieces, axes):
    return lax.all_to_all(pieces, axes, 0, 0, tiled=True)


def shared(value, axes):
    return exchange(jnp.broadcast_to(value, (lax.axis_size(axes), *value.shape)), axes)


def local(activations, upstream, weights):
    ch, co = activations.shape[0], upstream.shape[0]
    n_vox, n_y = lax.axis_size(VOX), lax.axis_size("y")
    n_xy, n_chan = lax.axis_size(XY), lax.axis_size(CHAN)
    cin = ch * n_chan
    up = [(i, i + 1) for i in range(n_vox - 1)]
    down = [(i + 1, i) for i in range(n_vox - 1)]
    act = activations.reshape(ch, PLANE)
    ups = upstream.reshape(co, PLANE)

    before = lax.ppermute(ups, VOX, up)
    after = lax.ppermute(ups, VOX, down)

    near = shared(act, "zl")

    w_rows = weights.transpose(1, 0, 2).reshape(27 * co, cin)
    part = backward(w_rows, jnp.stack([before, ups, after]))
    part = lax.psum_scatter(part.reshape(cin, PLANE), CHAN, scatter_dimension=0, tiled=True)
    input_grad = part.astype(BF16).reshape(ch, 1, PLANE)

    edge = jnp.where(lax.axis_index("x") == 0, before, after)
    planes = jnp.broadcast_to(jnp.concatenate([ups, edge]), (n_xy, 2 * co, PLANE))
    mixed = jnp.concatenate([near.reshape(n_xy, cin // (2 * n_xy), PLANE), planes], axis=1)
    mixed = exchange(mixed, XY)

    low = lax.all_gather(near[:, : ch // 2], "co", axis=0, tiled=False)
    high = lax.all_gather(near[:, ch // 2 :], "co", axis=0, tiled=False)
    around = forward(w_rows, low, high)
    after_part = lax.ppermute(around[2], VOX, down)
    before_part = lax.ppermute(around[0], VOX, up)
    outputs = (around[1] + after_part + before_part).astype(BF16).reshape(co, 1, PLANE)

    acts = shared(mixed[:, : cin // (2 * n_xy)], "co")
    raw = filter_grad(acts, mixed, n_y)
    raw = exchange(raw, "zh")
    raw = jnp.sum(raw, axis=0)
    scale = 1.0 / jnp.sqrt(jnp.float32(n_vox * PLANE))
    mine = (raw * scale).astype(BF16)
    halves = shared(mine, "zh")
    pieces = shared(halves, XY)
    weight_grad = join(pieces).transpose(1, 0, 2)
    return (outputs, input_grad, weight_grad)


def solution(mesh):
    finer = Mesh(mesh.devices.reshape(SPLIT), ("y", "zh", "x", "zl", "co"))
    specs = (P(CHAN, VOX, None), P(CHAN, VOX, None), P(CHAN, None, None))

    return jax.shard_map(local, mesh=finer, in_specs=specs, out_specs=specs, check_vma=False)


SPLIT = (4, 2, 4, 8, 2)
```

time: 204 us -> 188 us (0.922)
  the two profiles are of different devices: /device:TPU:454 before, /device:TPU:22 now
where the time goes in v3:
time: 188 us; the launch traced here: 187 us
  blocking collectives  67.2 us (36%)
  starting transfers between devices  53.2 us (28%)
  waiting for transfers between devices  28.2 us (15%)
  Pallas kernels  14.2 us (8%)
  between operations  14.2 us (8%)
  local copies, waits for them, and re-layouts  7.06 us (4%)
  other arithmetic  3.12 us (2%)
    all_to_all x4, blocking collectives, exchange(): return lax.all_to_all(pieces, axes, 0, 0, tiled=True)  62.9 us
    all_to_all x2, starting transfers between devices, exchange(): return lax.all_to_all(pieces, axes, 0, 0, tiled=True)  30.7 us
    ppermute x1, starting transfers between devices, local(): before = lax.ppermute(ups, VOX, up)  13.9 us
    all_to_all x2, waiting for transfers between devices, exchange(): return lax.all_to_all(pieces, axes, 0, 0, tiled=True)  8.52 us
    ppermute x1, waiting for transfers between devices, local(): before_part = lax.ppermute(around[0], VOX, up)  7.93 us
    pallas_call x1, Pallas kernels, join(): pl.pallas_call(join_kernel, grid=(9,), in_specs=[pl.BlockSpec((size, halv...  6.42 us
    ppermute x1, waiting for transfers between devices, local(): after_part = lax.ppermute(around[2], VOX, down)  5.45 us
    reduce_scatter x1, waiting for transfers between devices, local(): lax.psum_scatter(part.reshape(cin, PLANE), CHAN, scatter_dimension=0, til...  4.39 us
  transfers between devices with their start and end apart: 7, of which 6 were waited for; matrix products, arithmetic and copies ran while one was open for 3% of the time, Pallas kernels for 4%

profile of v3, /device:TPU:22, one launch (start us, length us, event | category | flops | bytes accessed | tf_op | source)
XLA Modules:
  0.0 187.2 jit_solution(15308629497613635291)
XLA Ops:
  7.2 1.8 broadcast_in_dim.15
  9.0 12.5 %all-to-all-start = ((bf16[8,64,512]{2,1,0:T(8,128)(2,1)}), bf16[8,64,512]{2,1,0:T(8,128)(2,1)S(1)}, u32[]{:S(2)}, u32[]{:S(2)}) async-start(bf16[8,64,512]{2,1,0:T(8,128)(2,1)} %broadcast_in_dim.15), calls=%async_computation | async-start | bytes 1048576 | tf_op jit(solution)/shard_map/all_to_all | solution.py:189
  21.5 2.7 %collective-permute-start.3 = (bf16[32,512]{1,0:T(8,128)(2,1)}, bf16[32,512]{1,0:T(8,128)(2,1)S(1)}, u32[]{:S(2)}, u32[]{:S(2)}) collective-permute-start(bf16[32,512]{1,0:T(8,128)(2,1)} %bitcast.39), channel_id=1, source_target_pairs={{16,0},{32,16},{48,32},{64,48},{80,64},{96,80},{112,96},{128,112},... | collective-permute-start | bytes 98312 | tf_op jit(solution)/shard_map/ppermute | solution.py:207
  24.3 13.9 %collective-permute-start.2 = (bf16[32,512]{1,0:T(8,128)(2,1)}, bf16[32,512]{1,0:T(8,128)(2,1)S(1)}, u32[]{:S(2)}, u32[]{:S(2)}) collective-permute-start(bf16[32,512]{1,0:T(8,128)(2,1)} %bitcast.40), channel_id=1, source_target_pairs={{0,16},{16,32},{32,48},{48,64},{64,80},{80,96},{96,112},{112,128},... | collective-permute-start | bytes 98312 | tf_op jit(solution)/shard_map/ppermute | solution.py:206
  40.9 2.9 %backward_plane.1 = f32[8,128,512]{2,1,0:T(8,128)} custom-call(bf16[864,1024]{1,0:T(8,128)(2,1)S(1)} %bitcast.31, bf16[3,32,512]{2,1,0:T(8,128)(2,1)S(1)} %pad_maximum_fusion.1.u_ref), custom_call_target="tpu_custom_call" | custom-call | tf_op jit(solution)/shard_map/backward_plane/pallas_call | solution.py:83
  44.5 8.5 %all-to-all-done = bf16[8,64,512]{2,1,0:T(8,128)(2,1)S(1)} async-done(((bf16[8,64,512]{2,1,0:T(8,128)(2,1)}), bf16[8,64,512]{2,1,0:T(8,128)(2,1)S(1)}, u32[]{:S(2)}, u32[]{:S(2)}) %all-to-all-start) | async-done | bytes 524320 | tf_op jit(solution)/shard_map/all_to_all | solution.py:189
  53.8 22.7 %all_to_all.30.u_ref = bf16[16,96,512]{2,1,0:T(8,128)(2,1)S(1)} all-to-all(bf16[16,96,512]{2,1,0:T(8,128)(2,1)S(1)} %pad_maximum_fusion), channel_id=1, replica_groups=mesh['y'=4,'zh'=2,'x'=4,'zl'=8,'co'=2] {'y','x'}, dimensions={0} | all-to-all | bytes 3145728 | tf_op jit(solution)/shard_map/all_to_all | solution.py:189
  76.7 4.6 %all_to_all.31.a_ref = bf16[2,16,32,512]{3,2,1,0:T(8,128)(2,1)S(1)} all-to-all(bf16[2,16,32,512]{3,2,1,0:T(8,128)(2,1)S(1)} %broadcast_in_dim.17), channel_id=1, replica_groups=mesh['y'=4,'zh'=2,'x'=4,'zl'=8,'co'=2] {'co'}, dimensions={0} | all-to-all | bytes 2097152 | tf_op jit(solution)/shard_map/all_to_all | solution.py:189
  81.3 3.7 %filter_planes.1 = f32[2,27,8,128]{3,2,1,0:T(8,128)S(1)} custom-call(bf16[2,16,32,512]{3,2,1,0:T(8,128)(2,1)S(1)} %all_to_all.31.a_ref, bf16[16,96,512]{2,1,0:T(8,128)(2,1)S(1)} %all_to_all.30.u_ref), custom_call_target="tpu_custom_call" | custom-call | tf_op jit(solution)/shard_map/filter_planes/pallas_call | solution.py:144
  85.0 19.1 %all_to_all.32 = f32[2,27,8,128]{3,2,1,0:T(8,128)S(1)} all-to-all(f32[2,27,8,128]{3,2,1,0:T(8,128)S(1)} %filter_planes.1), channel_id=1, replica_groups=mesh['y'=4,'zh'=2,'x'=4,'zl'=8,'co'=2] {'zh'}, dimensions={0} | all-to-all | bytes 442368 | tf_op jit(solution)/shard_map/all_to_all | solution.py:189
  104.2 16.4 %all_to_all.33 = bf16[2,27,8,128]{3,2,1,0:T(8,128)(2,1)S(1)} all-to-all(bf16[2,27,8,128]{3,2,1,0:T(8,128)(2,1)S(1)} %broadcast_in_dim.18), channel_id=1, replica_groups=mesh['y'=4,'zh'=2,'x'=4,'zl'=8,'co'=2] {'zh'}, dimensions={0} | all-to-all | bytes 221184 | tf_op jit(solution)/shard_map/all_to_all | solution.py:189
  120.6 1.4 broadcast_in_dim.19
  122.1 18.2 %all-to-all-start.5 = ((bf16[16,2,27,8,128]{4,3,2,1,0:T(8,128)(2,1)}), bf16[16,2,27,8,128]{4,3,2,1,0:T(8,128)(2,1)S(1)}, u32[]{:S(2)}, u32[]{:S(2)}) async-start(bf16[16,2,27,8,128]{4,3,2,1,0:T(8,128)(2,1)} %broadcast_in_dim.19), calls=%async_computation.6 | async-start | bytes 3538944 | tf_op jit(solution)/shard_map/all_to_all | solution.py:189
  141.3 2.2 %all-gather = bf16[16,32,512]{2,1,0:T(8,128)(2,1)S(1)} all-gather(bf16[8,32,512]{2,1,0:T(8,128)(2,1)S(1)} %get-tuple-element.4), channel_id=2, replica_groups=mesh['y'=4,'zh'=2,'x'=4,'zl'=8,'co'=2] {'co'}, dimensions={0}, use_global_device_ids=true | all-gather | bytes 786432 | tf_op jit(solution)/shard_map/all_gather | solution.py:221
  143.5 2.2 %all-gather.1 = bf16[16,32,512]{2,1,0:T(8,128)(2,1)S(1)} all-gather(bf16[8,32,512]{2,1,0:T(8,128)(2,1)S(1)} %get-tuple-element.3), channel_id=3, replica_groups=mesh['y'=4,'zh'=2,'x'=4,'zl'=8,'co'=2] {'co'}, dimensions={0}, use_global_device_ids=true | all-gather | bytes 786432 | tf_op jit(solution)/shard_map/all_gather | solution.py:222
  145.6 1.2 forward_plane.1
  146.9 1.9 %collective-permute-start.1 = (f32[32,512]{1,0:T(8,128)S(1)}, f32[32,512]{1,0:T(8,128)S(1)}, u32[]{:S(2)}, u32[]{:S(2)}) collective-permute-start(f32[32,512]{1,0:T(8,128)S(1)} %get-tuple-element.6), channel_id=1, source_target_pairs={{0,16},{16,32},{32,48},{48,64},{64,80},{80,96},{96,112},{112,128},... | collective-permute-start | bytes 196616 | tf_op jit(solution)/shard_map/ppermute | solution.py:225
  148.8 3.9 %collective-permute-start = (f32[32,512]{1,0:T(8,128)S(1)}, f32[32,512]{1,0:T(8,128)S(1)}, u32[]{:S(2)}, u32[]{:S(2)}) collective-permute-start(f32[32,512]{1,0:T(8,128)S(1)} %get-tuple-element.5), channel_id=1, source_target_pairs={{16,0},{32,16},{48,32},{64,48},{80,64},{96,80},{112,96},{128,112},... | collective-permute-start | bytes 196616 | tf_op jit(solution)/shard_map/ppermute | solution.py:224
  152.7 7.9 %collective-permute-done.1 = f32[32,512]{1,0:T(8,128)S(1)} collective-permute-done((f32[32,512]{1,0:T(8,128)S(1)}, f32[32,512]{1,0:T(8,128)S(1)}, u32[]{:S(2)}, u32[]{:S(2)}) %collective-permute-start.1) | collective-permute-done | bytes 65568 | tf_op jit(solution)/shard_map/ppermute | solution.py:225
  160.7 5.4 %collective-permute-done = f32[32,512]{1,0:T(8,128)S(1)} collective-permute-done((f32[32,512]{1,0:T(8,128)S(1)}, f32[32,512]{1,0:T(8,128)S(1)}, u32[]{:S(2)}, u32[]{:S(2)}) %collective-permute-start) | collective-permute-done | bytes 65568 | tf_op jit(solution)/shard_map/ppermute | solution.py:224
  166.8 4.4 %reduce-scatter.2.cloned.1.call-done = f32[64,512]{1,0:T(8,128)} async-done(((f32[1024,512]{1,0:T(8,128)}), f32[64,512]{1,0:T(8,128)}) %reduce-scatter.2.cloned.1.call-update) | async-done | bytes 131088 | tf_op jit(solution)/shard_map/reduce_scatter | solution.py:213
  171.1 1.5 convert_bitcast_fusion
  172.7 1.2 copy-done.1
  173.9 6.4 %join_pieces.1 = bf16[27,32,1024]{2,1,0:T(8,128)(2,1)} custom-call(bf16[16,2,27,8,128]{4,3,2,1,0:T(8,128)(2,1)} %copy-done.1), custom_call_target="tpu_custom_call" | custom-call | tf_op jit(solution)/shard_map/join_pieces/pallas_call | solution.py:178
  (25 shorter events, 6.1 us)
Async XLA Ops:
  7.2 33.7 %copy-start = (bf16[32,27,1024]{2,0,1:T(8,128)(2,1)S(1)}, bf16[32,27,1024]{2,0,1:T(8,128)(2,1)}, u32[]{:S(2)}) copy-start(bf16[32,27,1024]{2,0,1:T(8,128)(2,1)} %param.5) | copy-start | bytes 5308420
  9.0 44.1 %all-to-all-start = ((bf16[8,64,512]{2,1,0:T(8,128)(2,1)}), bf16[8,64,512]{2,1,0:T(8,128)(2,1)S(1)}, u32[]{:S(2)}, u32[]{:S(2)}) async-start(bf16[8,64,512]{2,1,0:T(8,128)(2,1)} %broadcast_in_dim.15), calls=%async_computation | async-start | bytes 1048576 | tf_op jit(solution)/shard_map/all_to_all | solution.py:189
  21.5 149.6 %reduce-scatter.2.cloned.1.call-start = ((), (), s32[]{:S(2)}) async-start(), calls=%async_computation.7 | async-start | bytes 2228224 | tf_op jit(solution)/shard_map/reduce_scatter | solution.py:213
  21.5 17.5 %collective-permute-start.3 = (bf16[32,512]{1,0:T(8,128)(2,1)}, bf16[32,512]{1,0:T(8,128)(2,1)S(1)}, u32[]{:S(2)}, u32[]{:S(2)}) collective-permute-start(bf16[32,512]{1,0:T(8,128)(2,1)} %bitcast.39), channel_id=1, source_target_pairs={{16,0},{32,16},{48,32},{64,48},{80,64},{96,80},{112,96},{128,112},... | collective-permute-start | bytes 98312 | tf_op jit(solution)/shard_map/ppermute | solution.py:207
  24.3 15.8 %collective-permute-start.2 = (bf16[32,512]{1,0:T(8,128)(2,1)}, bf16[32,512]{1,0:T(8,128)(2,1)S(1)}, u32[]{:S(2)}, u32[]{:S(2)}) collective-permute-start(bf16[32,512]{1,0:T(8,128)(2,1)} %bitcast.40), channel_id=1, source_target_pairs={{0,16},{16,32},{32,48},{48,64},{64,80},{80,96},{96,112},{112,128},... | collective-permute-start | bytes 98312 | tf_op jit(solution)/shard_map/ppermute | solution.py:206
  43.8 0.8 copy-start.3
  53.0 0.8 copy-start.2
  122.1 50.6 %all-to-all-start.5 = ((bf16[16,2,27,8,128]{4,3,2,1,0:T(8,128)(2,1)}), bf16[16,2,27,8,128]{4,3,2,1,0:T(8,128)(2,1)S(1)}, u32[]{:S(2)}, u32[]{:S(2)}) async-start(bf16[16,2,27,8,128]{4,3,2,1,0:T(8,128)(2,1)} %broadcast_in_dim.19), calls=%async_computation.6 | async-start | bytes 3538944 | tf_op jit(solution)/shard_map/all_to_all | solution.py:189
  146.9 13.8 %collective-permute-start.1 = (f32[32,512]{1,0:T(8,128)S(1)}, f32[32,512]{1,0:T(8,128)S(1)}, u32[]{:S(2)}, u32[]{:S(2)}) collective-permute-start(f32[32,512]{1,0:T(8,128)S(1)} %get-tuple-element.6), channel_id=1, source_target_pairs={{0,16},{16,32},{32,48},{48,64},{64,80},{80,96},{96,112},{112,128},... | collective-permute-start | bytes 196616 | tf_op jit(solution)/shard_map/ppermute | solution.py:225
  148.8 17.3 %collective-permute-start = (f32[32,512]{1,0:T(8,128)S(1)}, f32[32,512]{1,0:T(8,128)S(1)}, u32[]{:S(2)}, u32[]{:S(2)}) collective-permute-start(f32[32,512]{1,0:T(8,128)S(1)} %get-tuple-element.5), channel_id=1, source_target_pairs={{16,0},{32,16},{48,32},{64,48},{80,64},{96,80},{112,96},{128,112},... | collective-permute-start | bytes 196616 | tf_op jit(solution)/shard_map/ppermute | solution.py:224
  172.7 1.2 copy-start.1
Sparse Core Ops, SparseCore 0:
  43.9 127.1 reduce-scatter.1

commit v4 on v3

--- a/solution.py
+++ b/solution.py
@@ -177,10 +177,11 @@
     size, halves = pieces.shape[:2]
     return pl.pallas_call(
         join_kernel,
-        grid=(9,),
-        in_specs=[pl.BlockSpec((size, halves, 3, 8, 128), lambda g: (0, 0, g, 0, 0))],
-        out_specs=pl.BlockSpec((3, 16 * halves, 64 * size), lambda g: (g, 0, 0)),
+        grid=(3,),
+        in_specs=[pl.BlockSpec((size, halves, 9, 8, 128), lambda g: (0, 0, g, 0, 0))],
+        out_specs=pl.BlockSpec((9, 16 * halves, 64 * size), lambda g: (g, 0, 0)),
         out_shape=jax.ShapeDtypeStruct((27, 16 * halves, 64 * size), BF16),
+        compiler_params=pltpu.CompilerParams(vmem_limit_bytes=16 * 2**20),
         name="join_pieces",
     )(pieces)
 

time: 188 us -> 183 us (0.973)
  Pallas kernels: 14.2 us -> 10 us
    pallas_call x1, Pallas kernels: 6.42 us -> 2.26 us  [join(): pl.pallas_call(join_kernel, grid=(3,), in_specs=[pl.BlockSpec((size, halv...]
where the time goes in v4:
time: 183 us; the launch traced here: 182 us
  blocking collectives  67.1 us (37%)
  starting transfers between devices  53.4 us (29%)
  waiting for transfers between devices  28.3 us (15%)
  between operations  14.2 us (8%)
  Pallas kernels  10 us (5%)
  local copies, waits for them, and re-layouts  5.85 us (3%)
  other arithmetic  3.12 us (2%)
    all_to_all x4, blocking collectives, exchange(): return lax.all_to_all(pieces, axes, 0, 0, tiled=True)  62.7 us
    all_to_all x2, starting transfers between devices, exchange(): return lax.all_to_all(pieces, axes, 0, 0, tiled=True)  30.8 us
    ppermute x1, starting transfers between devices, local(): before = lax.ppermute(ups, VOX, up)  13.9 us
    all_to_all x2, waiting for transfers between devices, exchange(): return lax.all_to_all(pieces, axes, 0, 0, tiled=True)  8.52 us
    ppermute x1, waiting for transfers between devices, local(): after_part = lax.ppermute(around[2], VOX, down)  7.03 us
    ppermute x1, waiting for transfers between devices, local(): before_part = lax.ppermute(around[0], VOX, up)  6.21 us
    reduce_scatter x1, waiting for transfers between devices, local(): lax.psum_scatter(part.reshape(cin, PLANE), CHAN, scatter_dimension=0, til...  4.6 us
    ppermute x1, starting transfers between devices, local(): after_part = lax.ppermute(around[2], VOX, down)  3.92 us
  transfers between devices with their start and end apart: 7, of which 6 were waited for; matrix products, arithmetic and copies ran while one was open for 3% of the time, Pallas kernels for 4%

profile of v4, /device:TPU:22, one launch (start us, length us, event | category | flops | bytes accessed | tf_op | source)
XLA Modules:
  0.0 181.9 jit_solution(14398566012724612158)
XLA Ops:
  7.2 1.8 broadcast_in_dim.15
  9.0 12.5 %all-to-all-start = ((bf16[8,64,512]{2,1,0:T(8,128)(2,1)}), bf16[8,64,512]{2,1,0:T(8,128)(2,1)S(1)}, u32[]{:S(2)}, u32[]{:S(2)}) async-start(bf16[8,64,512]{2,1,0:T(8,128)(2,1)} %broadcast_in_dim.15), calls=%async_computation | async-start | bytes 1048576 | tf_op jit(solution)/shard_map/all_to_all | solution.py:190
  21.5 2.7 %collective-permute-start.3 = (bf16[32,512]{1,0:T(8,128)(2,1)}, bf16[32,512]{1,0:T(8,128)(2,1)S(1)}, u32[]{:S(2)}, u32[]{:S(2)}) collective-permute-start(bf16[32,512]{1,0:T(8,128)(2,1)} %bitcast.39), channel_id=1, source_target_pairs={{16,0},{32,16},{48,32},{64,48},{80,64},{96,80},{112,96},{128,112},... | collective-permute-start | bytes 98312 | tf_op jit(solution)/shard_map/ppermute | solution.py:208
  24.3 13.9 %collective-permute-start.2 = (bf16[32,512]{1,0:T(8,128)(2,1)}, bf16[32,512]{1,0:T(8,128)(2,1)S(1)}, u32[]{:S(2)}, u32[]{:S(2)}) collective-permute-start(bf16[32,512]{1,0:T(8,128)(2,1)} %bitcast.40), channel_id=1, source_target_pairs={{0,16},{16,32},{32,48},{48,64},{64,80},{80,96},{96,112},{112,128},... | collective-permute-start | bytes 98312 | tf_op jit(solution)/shard_map/ppermute | solution.py:207
  40.9 2.9 %backward_plane.1 = f32[8,128,512]{2,1,0:T(8,128)} custom-call(bf16[864,1024]{1,0:T(8,128)(2,1)S(1)} %bitcast.31, bf16[3,32,512]{2,1,0:T(8,128)(2,1)S(1)} %pad_maximum_fusion.1.u_ref), custom_call_target="tpu_custom_call" | custom-call | tf_op jit(solution)/shard_map/backward_plane/pallas_call | solution.py:83
  44.5 8.5 %all-to-all-done = bf16[8,64,512]{2,1,0:T(8,128)(2,1)S(1)} async-done(((bf16[8,64,512]{2,1,0:T(8,128)(2,1)}), bf16[8,64,512]{2,1,0:T(8,128)(2,1)S(1)}, u32[]{:S(2)}, u32[]{:S(2)}) %all-to-all-start) | async-done | bytes 524320 | tf_op jit(solution)/shard_map/all_to_all | solution.py:190
  53.9 22.7 %all_to_all.30.u_ref = bf16[16,96,512]{2,1,0:T(8,128)(2,1)S(1)} all-to-all(bf16[16,96,512]{2,1,0:T(8,128)(2,1)S(1)} %pad_maximum_fusion), channel_id=1, replica_groups=mesh['y'=4,'zh'=2,'x'=4,'zl'=8,'co'=2] {'y','x'}, dimensions={0} | all-to-all | bytes 3145728 | tf_op jit(solution)/shard_map/all_to_all | solution.py:190
  76.7 4.6 %all_to_all.31.a_ref = bf16[2,16,32,512]{3,2,1,0:T(8,128)(2,1)S(1)} all-to-all(bf16[2,16,32,512]{3,2,1,0:T(8,128)(2,1)S(1)} %broadcast_in_dim.17), channel_id=1, replica_groups=mesh['y'=4,'zh'=2,'x'=4,'zl'=8,'co'=2] {'co'}, dimensions={0} | all-to-all | bytes 2097152 | tf_op jit(solution)/shard_map/all_to_all | solution.py:190
  81.4 3.7 %filter_planes.1 = f32[2,27,8,128]{3,2,1,0:T(8,128)S(1)} custom-call(bf16[2,16,32,512]{3,2,1,0:T(8,128)(2,1)S(1)} %all_to_all.31.a_ref, bf16[16,96,512]{2,1,0:T(8,128)(2,1)S(1)} %all_to_all.30.u_ref), custom_call_target="tpu_custom_call" | custom-call | tf_op jit(solution)/shard_map/filter_planes/pallas_call | solution.py:144
  85.1 19.2 %all_to_all.32 = f32[2,27,8,128]{3,2,1,0:T(8,128)S(1)} all-to-all(f32[2,27,8,128]{3,2,1,0:T(8,128)S(1)} %filter_planes.1), channel_id=1, replica_groups=mesh['y'=4,'zh'=2,'x'=4,'zl'=8,'co'=2] {'zh'}, dimensions={0} | all-to-all | bytes 442368 | tf_op jit(solution)/shard_map/all_to_all | solution.py:190
  104.3 16.2 %all_to_all.33 = bf16[2,27,8,128]{3,2,1,0:T(8,128)(2,1)S(1)} all-to-all(bf16[2,27,8,128]{3,2,1,0:T(8,128)(2,1)S(1)} %broadcast_in_dim.18), channel_id=1, replica_groups=mesh['y'=4,'zh'=2,'x'=4,'zl'=8,'co'=2] {'zh'}, dimensions={0} | all-to-all | bytes 221184 | tf_op jit(solution)/shard_map/all_to_all | solution.py:190
  120.5 1.4 broadcast_in_dim.19
  122.0 18.3 %all-to-all-start.5 = ((bf16[16,2,27,8,128]{4,3,2,1,0:T(8,128)(2,1)}), bf16[16,2,27,8,128]{4,3,2,1,0:T(8,128)(2,1)S(1)}, u32[]{:S(2)}, u32[]{:S(2)}) async-start(bf16[16,2,27,8,128]{4,3,2,1,0:T(8,128)(2,1)} %broadcast_in_dim.19), calls=%async_computation.6 | async-start | bytes 3538944 | tf_op jit(solution)/shard_map/all_to_all | solution.py:190
  140.3 1.1 fusion.4
  141.3 2.2 %all-gather = bf16[16,32,512]{2,1,0:T(8,128)(2,1)S(1)} all-gather(bf16[8,32,512]{2,1,0:T(8,128)(2,1)S(1)} %get-tuple-element.4), channel_id=2, replica_groups=mesh['y'=4,'zh'=2,'x'=4,'zl'=8,'co'=2] {'co'}, dimensions={0}, use_global_device_ids=true | all-gather | bytes 786432 | tf_op jit(solution)/shard_map/all_gather | solution.py:222
  143.5 2.2 %all-gather.1 = bf16[16,32,512]{2,1,0:T(8,128)(2,1)S(1)} all-gather(bf16[8,32,512]{2,1,0:T(8,128)(2,1)S(1)} %get-tuple-element.3), channel_id=3, replica_groups=mesh['y'=4,'zh'=2,'x'=4,'zl'=8,'co'=2] {'co'}, dimensions={0}, use_global_device_ids=true | all-gather | bytes 786432 | tf_op jit(solution)/shard_map/all_gather | solution.py:223
  145.7 1.2 forward_plane.1
  146.9 1.9 %collective-permute-start.1 = (f32[32,512]{1,0:T(8,128)S(1)}, f32[32,512]{1,0:T(8,128)S(1)}, u32[]{:S(2)}, u32[]{:S(2)}) collective-permute-start(f32[32,512]{1,0:T(8,128)S(1)} %get-tuple-element.6), channel_id=1, source_target_pairs={{0,16},{16,32},{32,48},{48,64},{64,80},{80,96},{96,112},{112,128},... | collective-permute-start | bytes 196616 | tf_op jit(solution)/shard_map/ppermute | solution.py:226
  148.9 3.9 %collective-permute-start = (f32[32,512]{1,0:T(8,128)S(1)}, f32[32,512]{1,0:T(8,128)S(1)}, u32[]{:S(2)}, u32[]{:S(2)}) collective-permute-start(f32[32,512]{1,0:T(8,128)S(1)} %get-tuple-element.5), channel_id=1, source_target_pairs={{16,0},{32,16},{48,32},{64,48},{80,64},{96,80},{112,96},{128,112},... | collective-permute-start | bytes 196616 | tf_op jit(solution)/shard_map/ppermute | solution.py:225
  152.8 6.2 %collective-permute-done.1 = f32[32,512]{1,0:T(8,128)S(1)} collective-permute-done((f32[32,512]{1,0:T(8,128)S(1)}, f32[32,512]{1,0:T(8,128)S(1)}, u32[]{:S(2)}, u32[]{:S(2)}) %collective-permute-start.1) | collective-permute-done | bytes 65568 | tf_op jit(solution)/shard_map/ppermute | solution.py:226
  159.0 7.0 %collective-permute-done = f32[32,512]{1,0:T(8,128)S(1)} collective-permute-done((f32[32,512]{1,0:T(8,128)S(1)}, f32[32,512]{1,0:T(8,128)S(1)}, u32[]{:S(2)}, u32[]{:S(2)}) %collective-permute-start) | collective-permute-done | bytes 65568 | tf_op jit(solution)/shard_map/ppermute | solution.py:225
  166.6 4.6 %reduce-scatter.2.cloned.1.call-done = f32[64,512]{1,0:T(8,128)} async-done(((f32[1024,512]{1,0:T(8,128)}), f32[64,512]{1,0:T(8,128)}) %reduce-scatter.2.cloned.1.call-update) | async-done | bytes 131088 | tf_op jit(solution)/shard_map/reduce_scatter | solution.py:214
  171.3 1.5 convert_bitcast_fusion
  172.8 2.3 %join_pieces.1 = bf16[27,32,1024]{2,1,0:T(8,128)(2,1)} custom-call(bf16[16,2,27,8,128]{4,3,2,1,0:T(8,128)(2,1)S(1)} %all-to-all-done.5.r_ref), custom_call_target="tpu_custom_call" | custom-call | tf_op jit(solution)/shard_map/join_pieces/pallas_call | solution.py:178
  (23 shorter events, 5.1 us)
Async XLA Ops:
  7.2 33.7 %copy-start = (bf16[32,27,1024]{2,0,1:T(8,128)(2,1)S(1)}, bf16[32,27,1024]{2,0,1:T(8,128)(2,1)}, u32[]{:S(2)}) copy-start(bf16[32,27,1024]{2,0,1:T(8,128)(2,1)} %param.5) | copy-start | bytes 5308420
  9.0 44.1 %all-to-all-start = ((bf16[8,64,512]{2,1,0:T(8,128)(2,1)}), bf16[8,64,512]{2,1,0:T(8,128)(2,1)S(1)}, u32[]{:S(2)}, u32[]{:S(2)}) async-start(bf16[8,64,512]{2,1,0:T(8,128)(2,1)} %broadcast_in_dim.15), calls=%async_computation | async-start | bytes 1048576 | tf_op jit(solution)/shard_map/all_to_all | solution.py:190
  21.5 149.7 %reduce-scatter.2.cloned.1.call-start = ((), (), s32[]{:S(2)}) async-start(), calls=%async_computation.7 | async-start | bytes 2228224 | tf_op jit(solution)/shard_map/reduce_scatter | solution.py:214
  21.5 17.5 %collective-permute-start.3 = (bf16[32,512]{1,0:T(8,128)(2,1)}, bf16[32,512]{1,0:T(8,128)(2,1)S(1)}, u32[]{:S(2)}, u32[]{:S(2)}) collective-permute-start(bf16[32,512]{1,0:T(8,128)(2,1)} %bitcast.39), channel_id=1, source_target_pairs={{16,0},{32,16},{48,32},{64,48},{80,64},{96,80},{112,96},{128,112},... | collective-permute-start | bytes 98312 | tf_op jit(solution)/shard_map/ppermute | solution.py:208
  24.3 15.8 %collective-permute-start.2 = (bf16[32,512]{1,0:T(8,128)(2,1)}, bf16[32,512]{1,0:T(8,128)(2,1)S(1)}, u32[]{:S(2)}, u32[]{:S(2)}) collective-permute-start(bf16[32,512]{1,0:T(8,128)(2,1)} %bitcast.40), channel_id=1, source_target_pairs={{0,16},{16,32},{32,48},{48,64},{64,80},{80,96},{96,112},{112,128},... | collective-permute-start | bytes 98312 | tf_op jit(solution)/shard_map/ppermute | solution.py:207
  43.8 0.8 copy-start.2
  53.0 0.8 copy-start.1
  122.0 50.8 %all-to-all-start.5 = ((bf16[16,2,27,8,128]{4,3,2,1,0:T(8,128)(2,1)}), bf16[16,2,27,8,128]{4,3,2,1,0:T(8,128)(2,1)S(1)}, u32[]{:S(2)}, u32[]{:S(2)}) async-start(bf16[16,2,27,8,128]{4,3,2,1,0:T(8,128)(2,1)} %broadcast_in_dim.19), calls=%async_computation.6 | async-start | bytes 3538944 | tf_op jit(solution)/shard_map/all_to_all | solution.py:190
  146.9 12.1 %collective-permute-start.1 = (f32[32,512]{1,0:T(8,128)S(1)}, f32[32,512]{1,0:T(8,128)S(1)}, u32[]{:S(2)}, u32[]{:S(2)}) collective-permute-start(f32[32,512]{1,0:T(8,128)S(1)} %get-tuple-element.6), channel_id=1, source_target_pairs={{0,16},{16,32},{32,48},{48,64},{64,80},{80,96},{96,112},{112,128},... | collective-permute-start | bytes 196616 | tf_op jit(solution)/shard_map/ppermute | solution.py:226
  148.9 17.2 %collective-permute-start = (f32[32,512]{1,0:T(8,128)S(1)}, f32[32,512]{1,0:T(8,128)S(1)}, u32[]{:S(2)}, u32[]{:S(2)}) collective-permute-start(f32[32,512]{1,0:T(8,128)S(1)} %get-tuple-element.5), channel_id=1, source_target_pairs={{16,0},{32,16},{48,32},{64,48},{80,64},{96,80},{112,96},{128,112},... | collective-permute-start | bytes 196616 | tf_op jit(solution)/shard_map/ppermute | solution.py:225
Sparse Core Ops, SparseCore 0:
  43.9 127.2 reduce-scatter.1

commit v5 on v4

--- a/solution.py
+++ b/solution.py
@@ -71,18 +71,20 @@
             for c in range(3):
                 k = 9 * a + 3 * b + c
                 cols[rows * k : rows * (k + 1), :] = moved(plane, 1 - b, 1 - c).astype(BF16)
-    ch = o_ref.shape[1]
-    for t in range(o_ref.shape[0]):
-        part = w_ref[:, ch * t : ch * (t + 1)]
-        o_ref[t] = lax.dot_general(part, cols[...], (((0,), (0,)), ((), ())), preferred_element_type=F32)
-
-
-def backward(w_rows, planes):
+    cores, chips, ch = o_ref.shape[:3]
+    for t in range(chips):
+        part = w_ref[:, cores * ch * t : cores * ch * (t + 1)]
+        got = lax.dot_general(part, cols[...], (((0,), (0,)), ((), ())), preferred_element_type=F32)
+        for e in range(cores):
+            o_ref[e, t] = got[ch * e : ch * (e + 1)]
+
+
+def backward(w_rows, planes, cores, chips):
     width = w_rows.shape[1]
     rows = planes.shape[1]
     return pl.pallas_call(
         backward_kernel,
-        out_shape=jax.ShapeDtypeStruct((width // 128, 128, PLANE), F32),
+        out_shape=jax.ShapeDtypeStruct((cores, chips, width // (cores * chips), PLANE), F32),
         scratch_shapes=[pltpu.VMEM((27 * rows, PLANE), BF16)],
         compiler_params=pltpu.CompilerParams(vmem_limit_bytes=32 * 2**20),
         name="backward_plane",
@@ -210,8 +212,9 @@
     near = shared(act, "zl")
 
     w_rows = weights.transpose(1, 0, 2).reshape(27 * co, cin)
-    part = backward(w_rows, jnp.stack([before, ups, after]))
-    part = lax.psum_scatter(part.reshape(cin, PLANE), CHAN, scatter_dimension=0, tiled=True)
+    part = backward(w_rows, jnp.stack([before, ups, after]), lax.axis_size("co"), lax.axis_size("zl"))
+    part = lax.psum_scatter(part.reshape(cin, PLANE), "co", scatter_dimension=0, tiled=True)
+    part = lax.psum_scatter(part, "zl", scatter_dimension=0, tiled=True)
     input_grad = part.astype(BF16).reshape(ch, 1, PLANE)
 
     edge = jnp.where(lax.axis_index("x") == 0, before, after)

time: 183 us -> 208 us (1.14)
  the two profiles are of different devices: /device:TPU:22 before, /device:TPU:6 now
where the time goes in v5:
time: 208 us; the launch traced here: 207 us
  blocking collectives  76 us (37%)
  waiting for transfers between devices  57.8 us (28%)
  starting transfers between devices  41.4 us (20%)
  between operations  14.2 us (7%)
  Pallas kernels  10 us (5%)
  local copies, waits for them, and re-layouts  4.86 us (2%)
  other arithmetic  3.11 us (1%)
    all_to_all x4, blocking collectives, exchange(): return lax.all_to_all(pieces, axes, 0, 0, tiled=True)  71.6 us
    all_to_all x2, waiting for transfers between devices, exchange(): return lax.all_to_all(pieces, axes, 0, 0, tiled=True)  27.5 us
    all_to_all x2, starting transfers between devices, exchange(): return lax.all_to_all(pieces, axes, 0, 0, tiled=True)  17.9 us
    ppermute x1, starting transfers between devices, local(): before = lax.ppermute(ups, VOX, up)  14.8 us
    reduce_scatter x1, waiting for transfers between devices, local(): part = lax.psum_scatter(part, 'zl', scatter_dimension=0, tiled=True)  14.7 us
    ppermute x1, waiting for transfers between devices, local(): after_part = lax.ppermute(around[2], VOX, down)  9.18 us
    ppermute x1, waiting for transfers between devices, local(): before_part = lax.ppermute(around[0], VOX, up)  4.47 us
  transfers between devices with their start and end apart: 8, of which 6 were waited for; matrix products, arithmetic and copies ran while one was open for 2% of the time, Pallas kernels for 3%

profile of v5, /device:TPU:6, one launch (start us, length us, event | category | flops | bytes accessed | tf_op | source)
XLA Modules:
  0.0 207.5 jit_solution(7665019631486023360)
XLA Ops:
  7.2 2.7 %collective-permute-start.3 = (bf16[32,512]{1,0:T(8,128)(2,1)}, bf16[32,512]{1,0:T(8,128)(2,1)S(1)}, u32[]{:S(2)}, u32[]{:S(2)}) collective-permute-start(bf16[32,512]{1,0:T(8,128)(2,1)} %bitcast.39), channel_id=1, source_target_pairs={{16,0},{32,16},{48,32},{64,48},{80,64},{96,80},{112,96},{128,112},... | collective-permute-start | bytes 98312 | tf_op jit(solution)/shard_map/ppermute | solution.py:210
  10.0 14.8 %collective-permute-start.2 = (bf16[32,512]{1,0:T(8,128)(2,1)}, bf16[32,512]{1,0:T(8,128)(2,1)S(1)}, u32[]{:S(2)}, u32[]{:S(2)}) collective-permute-start(bf16[32,512]{1,0:T(8,128)(2,1)} %bitcast.40), channel_id=1, source_target_pairs={{0,16},{16,32},{32,48},{48,64},{64,80},{80,96},{96,112},{112,128},... | collective-permute-start | bytes 98312 | tf_op jit(solution)/shard_map/ppermute | solution.py:209
  25.1 1.6 collective-permute-done.2
  27.5 1.5 copy-done
  28.9 2.9 %backward_plane.1 = f32[2,8,64,512]{3,2,1,0:T(8,128)} custom-call(bf16[864,1024]{1,0:T(8,128)(2,1)S(1)} %bitcast.31, bf16[3,32,512]{2,1,0:T(8,128)(2,1)S(1)} %pad_maximum_fusion.1.u_ref), custom_call_target="tpu_custom_call" | custom-call | tf_op jit(solution)/shard_map/backward_plane/pallas_call | solution.py:85
  33.5 11.6 %all-to-all-start = ((bf16[8,64,512]{2,1,0:T(8,128)(2,1)}), bf16[8,64,512]{2,1,0:T(8,128)(2,1)S(1)}, u32[]{:S(2)}, u32[]{:S(2)}) async-start(bf16[8,64,512]{2,1,0:T(8,128)(2,1)} %broadcast_in_dim.15), calls=%async_computation | async-start | bytes 1048576 | tf_op jit(solution)/shard_map/all_to_all | solution.py:192
  45.2 27.5 %all-to-all-done = bf16[8,64,512]{2,1,0:T(8,128)(2,1)S(1)} async-done(((bf16[8,64,512]{2,1,0:T(8,128)(2,1)}), bf16[8,64,512]{2,1,0:T(8,128)(2,1)S(1)}, u32[]{:S(2)}, u32[]{:S(2)}) %all-to-all-start) | async-done | bytes 524320 | tf_op jit(solution)/shard_map/all_to_all | solution.py:192
  72.9 27.2 %all_to_all.30.u_ref = bf16[16,96,512]{2,1,0:T(8,128)(2,1)S(1)} all-to-all(bf16[16,96,512]{2,1,0:T(8,128)(2,1)S(1)} %pad_maximum_fusion), channel_id=1, replica_groups=mesh['y'=4,'zh'=2,'x'=4,'zl'=8,'co'=2] {'y','x'}, dimensions={0} | all-to-all | bytes 3145728 | tf_op jit(solution)/shard_map/all_to_all | solution.py:192
  100.3 4.6 %all_to_all.31.a_ref = bf16[2,16,32,512]{3,2,1,0:T(8,128)(2,1)S(1)} all-to-all(bf16[2,16,32,512]{3,2,1,0:T(8,128)(2,1)S(1)} %broadcast_in_dim.17), channel_id=1, replica_groups=mesh['y'=4,'zh'=2,'x'=4,'zl'=8,'co'=2] {'co'}, dimensions={0} | all-to-all | bytes 2097152 | tf_op jit(solution)/shard_map/all_to_all | solution.py:192
  104.9 3.7 %filter_planes.1 = f32[2,27,8,128]{3,2,1,0:T(8,128)S(1)} custom-call(bf16[2,16,32,512]{3,2,1,0:T(8,128)(2,1)S(1)} %all_to_all.31.a_ref, bf16[16,96,512]{2,1,0:T(8,128)(2,1)S(1)} %all_to_all.30.u_ref), custom_call_target="tpu_custom_call" | custom-call | tf_op jit(solution)/shard_map/filter_planes/pallas_call | solution.py:146
  108.6 23.8 %all_to_all.32 = f32[2,27,8,128]{3,2,1,0:T(8,128)S(1)} all-to-all(f32[2,27,8,128]{3,2,1,0:T(8,128)S(1)} %filter_planes.1), channel_id=1, replica_groups=mesh['y'=4,'zh'=2,'x'=4,'zl'=8,'co'=2] {'zh'}, dimensions={0} | all-to-all | bytes 442368 | tf_op jit(solution)/shard_map/all_to_all | solution.py:192
  132.5 16.0 %all_to_all.33 = bf16[2,27,8,128]{3,2,1,0:T(8,128)(2,1)S(1)} all-to-all(bf16[2,27,8,128]{3,2,1,0:T(8,128)(2,1)S(1)} %broadcast_in_dim.18), channel_id=1, replica_groups=mesh['y'=4,'zh'=2,'x'=4,'zl'=8,'co'=2] {'zh'}, dimensions={0} | all-to-all | bytes 221184 | tf_op jit(solution)/shard_map/all_to_all | solution.py:192
  148.5 1.4 broadcast_in_dim.19
  149.9 6.3 %all-to-all-start.5 = ((bf16[16,2,27,8,128]{4,3,2,1,0:T(8,128)(2,1)}), bf16[16,2,27,8,128]{4,3,2,1,0:T(8,128)(2,1)S(1)}, u32[]{:S(2)}, u32[]{:S(2)}) async-start(bf16[16,2,27,8,128]{4,3,2,1,0:T(8,128)(2,1)} %broadcast_in_dim.19), calls=%async_computation.7 | async-start | bytes 3538944 | tf_op jit(solution)/shard_map/all_to_all | solution.py:192
  156.3 2.3 %all-gather = bf16[16,32,512]{2,1,0:T(8,128)(2,1)S(1)} all-gather(bf16[8,32,512]{2,1,0:T(8,128)(2,1)S(1)} %get-tuple-element.4), channel_id=2, replica_groups=mesh['y'=4,'zh'=2,'x'=4,'zl'=8,'co'=2] {'co'}, dimensions={0}, use_global_device_ids=true | all-gather | bytes 786432 | tf_op jit(solution)/shard_map/all_gather | solution.py:225
  158.6 2.2 %all-gather.1 = bf16[16,32,512]{2,1,0:T(8,128)(2,1)S(1)} all-gather(bf16[8,32,512]{2,1,0:T(8,128)(2,1)S(1)} %get-tuple-element.3), channel_id=3, replica_groups=mesh['y'=4,'zh'=2,'x'=4,'zl'=8,'co'=2] {'co'}, dimensions={0}, use_global_device_ids=true | all-gather | bytes 786432 | tf_op jit(solution)/shard_map/all_gather | solution.py:226
  160.8 1.2 forward_plane.1
  162.0 1.9 collective-permute-start.1
  164.0 3.9 %collective-permute-start = (f32[32,512]{1,0:T(8,128)S(1)}, f32[32,512]{1,0:T(8,128)S(1)}, u32[]{:S(2)}, u32[]{:S(2)}) collective-permute-start(f32[32,512]{1,0:T(8,128)S(1)} %get-tuple-element.5), channel_id=1, source_target_pairs={{16,0},{32,16},{48,32},{64,48},{80,64},{96,80},{112,96},{128,112},... | collective-permute-start | bytes 196616 | tf_op jit(solution)/shard_map/ppermute | solution.py:228
  167.9 4.5 %collective-permute-done.1 = f32[32,512]{1,0:T(8,128)S(1)} collective-permute-done((f32[32,512]{1,0:T(8,128)S(1)}, f32[32,512]{1,0:T(8,128)S(1)}, u32[]{:S(2)}, u32[]{:S(2)}) %collective-permute-start.1) | collective-permute-done | bytes 65568 | tf_op jit(solution)/shard_map/ppermute | solution.py:229
  172.4 9.2 %collective-permute-done = f32[32,512]{1,0:T(8,128)S(1)} collective-permute-done((f32[32,512]{1,0:T(8,128)S(1)}, f32[32,512]{1,0:T(8,128)S(1)}, u32[]{:S(2)}, u32[]{:S(2)}) %collective-permute-start) | collective-permute-done | bytes 65568 | tf_op jit(solution)/shard_map/ppermute | solution.py:228
  182.2 2.3 %join_pieces.1 = bf16[27,32,1024]{2,1,0:T(8,128)(2,1)} custom-call(bf16[16,2,27,8,128]{4,3,2,1,0:T(8,128)(2,1)S(1)} %all-to-all-done.5.r_ref), custom_call_target="tpu_custom_call" | custom-call | tf_op jit(solution)/shard_map/join_pieces/pallas_call | solution.py:180
  184.4 14.7 %reduce-scatter.5.cloned.1.call-done = f32[64,512]{1,0:T(8,128)} async-done(((f32[512,512]{1,0:T(8,128)}), f32[64,512]{1,0:T(8,128)}) %reduce-scatter.5.cloned.1.call-update) | async-done | bytes 131088 | tf_op jit(solution)/shard_map/reduce_scatter | solution.py:217
  199.1 1.5 convert_bitcast_fusion
  (28 shorter events, 3.9 us)
Async XLA Ops:
  7.2 125.3 %reduce-scatter.3.cloned.1.call-start = ((), (), s32[]{:S(2)}) async-start(), calls=%async_computation.8 | async-start | bytes 3145728 | tf_op jit(solution)/shard_map/reduce_scatter | solution.py:216
  7.2 17.8 %collective-permute-start.3 = (bf16[32,512]{1,0:T(8,128)(2,1)}, bf16[32,512]{1,0:T(8,128)(2,1)S(1)}, u32[]{:S(2)}, u32[]{:S(2)}) collective-permute-start(bf16[32,512]{1,0:T(8,128)(2,1)} %bitcast.39), channel_id=1, source_target_pairs={{16,0},{32,16},{48,32},{64,48},{80,64},{96,80},{112,96},{128,112},... | collective-permute-start | bytes 98312 | tf_op jit(solution)/shard_map/ppermute | solution.py:210
  10.0 16.7 %collective-permute-start.2 = (bf16[32,512]{1,0:T(8,128)(2,1)}, bf16[32,512]{1,0:T(8,128)(2,1)S(1)}, u32[]{:S(2)}, u32[]{:S(2)}) collective-permute-start(bf16[32,512]{1,0:T(8,128)(2,1)} %bitcast.40), channel_id=1, source_target_pairs={{0,16},{16,32},{32,48},{48,64},{64,80},{80,96},{96,112},{112,128},... | collective-permute-start | bytes 98312 | tf_op jit(solution)/shard_map/ppermute | solution.py:209
  27.5 1.5 copy-start
  31.8 0.8 copy-start.3
  31.8 13.4 %copy-start.2 = (bf16[32,1,512]{2,0,1:T(8,128)(2,1)S(1)}, bf16[32,1,512]{2,0,1:T(8,128)(2,1)}, u32[]{:S(2)}) copy-start(bf16[32,1,512]{2,0,1:T(8,128)(2,1)} %param.4) | copy-start | bytes 98308
  33.5 39.2 %all-to-all-start = ((bf16[8,64,512]{2,1,0:T(8,128)(2,1)}), bf16[8,64,512]{2,1,0:T(8,128)(2,1)S(1)}, u32[]{:S(2)}, u32[]{:S(2)}) async-start(bf16[8,64,512]{2,1,0:T(8,128)(2,1)} %broadcast_in_dim.15), calls=%async_computation | async-start | bytes 1048576 | tf_op jit(solution)/shard_map/all_to_all | solution.py:192
  45.1 154.0 %reduce-scatter.5.cloned.1.call-start = ((), (), s32[]{:S(2)}) async-start(), calls=%async_computation.9 | async-start | bytes 1179648 | tf_op jit(solution)/shard_map/reduce_scatter | solution.py:217
  149.9 32.3 %all-to-all-start.5 = ((bf16[16,2,27,8,128]{4,3,2,1,0:T(8,128)(2,1)}), bf16[16,2,27,8,128]{4,3,2,1,0:T(8,128)(2,1)S(1)}, u32[]{:S(2)}, u32[]{:S(2)}) async-start(bf16[16,2,27,8,128]{4,3,2,1,0:T(8,128)(2,1)} %broadcast_in_dim.19), calls=%async_computation.7 | async-start | bytes 3538944 | tf_op jit(solution)/shard_map/all_to_all | solution.py:192
  156.3 4.5 %copy-start.1 = (bf16[32,27,1024]{2,0,1:T(8,128)(2,1)S(1)}, bf16[32,27,1024]{2,0,1:T(8,128)(2,1)}, u32[]{:S(2)}) copy-start(bf16[32,27,1024]{2,0,1:T(8,128)(2,1)} %param.5) | copy-start | bytes 5308420
  162.0 10.3 %collective-permute-start.1 = (f32[32,512]{1,0:T(8,128)S(1)}, f32[32,512]{1,0:T(8,128)S(1)}, u32[]{:S(2)}, u32[]{:S(2)}) collective-permute-start(f32[32,512]{1,0:T(8,128)S(1)} %get-tuple-element.6), channel_id=1, source_target_pairs={{0,16},{16,32},{32,48},{48,64},{64,80},{80,96},{96,112},{112,128},... | collective-permute-start | bytes 196616 | tf_op jit(solution)/shard_map/ppermute | solution.py:229
  164.0 17.6 %collective-permute-start = (f32[32,512]{1,0:T(8,128)S(1)}, f32[32,512]{1,0:T(8,128)S(1)}, u32[]{:S(2)}, u32[]{:S(2)}) collective-permute-start(f32[32,512]{1,0:T(8,128)S(1)} %get-tuple-element.5), channel_id=1, source_target_pairs={{16,0},{32,16},{48,32},{64,48},{80,64},{96,80},{112,96},{128,112},... | collective-permute-start | bytes 196616 | tf_op jit(solution)/shard_map/ppermute | solution.py:228
Sparse Core Ops, SparseCore 0:
  31.9 28.3 reduce-scatter.2
  132.6 66.4 reduce-scatter.4

commit v6 on v5

--- a/solution.py
+++ b/solution.py
@@ -162,30 +162,35 @@
     )(acts, mixed)
 
 
-def join_kernel(r_ref, o_ref):
+def join_kernel(own_ref, a_ref, b_ref, o_ref):
     even = lax.broadcasted_iota(jnp.int32, (8, 128), 1) // 32 % 2 == 0
-    for k in range(o_ref.shape[0]):
-        for t in range(r_ref.shape[0] // 2):
-            for h in range(r_ref.shape[1]):
-                left = r_ref[2 * t, h, k].astype(F32)
-                right = r_ref[2 * t + 1, h, k].astype(F32)
+    for ref, side in ((a_ref, own_ref[0]), (b_ref, 1 - own_ref[0])):
+        first = pl.multiple_of(16 * side, 16)
+        for k in range(o_ref.shape[0]):
+            for t in range(ref.shape[0] // 2):
+                left = ref[2 * t, k].astype(F32)
+                right = ref[2 * t + 1, k].astype(F32)
                 one = jnp.where(even, left, pltpu.roll(right, 32, 1))
                 two = jnp.where(even, pltpu.roll(left, 96, 1), right)
                 both = jnp.concatenate([one, two], axis=0).astype(BF16)
-                o_ref[k, 16 * h : 16 * (h + 1), 128 * t : 128 * (t + 1)] = both
-
-
-def join(pieces):
-    size, halves = pieces.shape[:2]
+                o_ref[k, pl.ds(first, 16), 128 * t : 128 * (t + 1)] = both
+
+
+def join(own, pieces, others):
+    size = pieces.shape[0]
+    block = pl.BlockSpec((size, 9, 8, 128), lambda g, own: (0, g, 0, 0))
     return pl.pallas_call(
         join_kernel,
-        grid=(3,),
-        in_specs=[pl.BlockSpec((size, halves, 9, 8, 128), lambda g: (0, 0, g, 0, 0))],
-        out_specs=pl.BlockSpec((9, 16 * halves, 64 * size), lambda g: (g, 0, 0)),
-        out_shape=jax.ShapeDtypeStruct((27, 16 * halves, 64 * size), BF16),
+        grid_spec=pltpu.PrefetchScalarGridSpec(
+            num_scalar_prefetch=1,
+            grid=(3,),
+            in_specs=[block, block],
+            out_specs=pl.BlockSpec((9, 32, 64 * size), lambda g, own: (g, 0, 0)),
+        ),
+        out_shape=jax.ShapeDtypeStruct((27, 32, 64 * size), BF16),
         compiler_params=pltpu.CompilerParams(vmem_limit_bytes=16 * 2**20),
         name="join_pieces",
-    )(pieces)
+    )(own, pieces, others)
 
 
 def exchange(pieces, axes):
@@ -229,15 +234,17 @@
     before_part = lax.ppermute(around[0], VOX, up)
     outputs = (around[1] + after_part + before_part).astype(BF16).reshape(co, 1, PLANE)
 
-    acts = shared(mixed[:, : cin // (2 * n_xy)], "co")
+    low_acts = mixed[:, : cin // (2 * n_xy)]
+    acts = shared(low_acts, "co")
     raw = filter_grad(acts, mixed, n_y)
     raw = exchange(raw, "zh")
     raw = jnp.sum(raw, axis=0)
     scale = 1.0 / jnp.sqrt(jnp.float32(n_vox * PLANE))
     mine = (raw * scale).astype(BF16)
-    halves = shared(mine, "zh")
-    pieces = shared(halves, XY)
-    weight_grad = join(pieces).transpose(1, 0, 2)
+    pieces = shared(mine, XY)
+    other = lax.ppermute(mine, "zh", [(0, 1), (1, 0)])
+    others = shared(other, XY)
+    weight_grad = join(lax.axis_index("zh").reshape(1), pieces, others).transpose(1, 0, 2)
     return (outputs, input_grad, weight_grad)
 
 

time: 208 us -> 212 us (1.019)
  the two profiles are of different devices: /device:TPU:6 before, /device:TPU:47 now
where the time goes in v6:
time: 212 us; the launch traced here: 211 us
  waiting for transfers between devices  76.7 us (36%)
  starting transfers between devices  53.4 us (25%)
  blocking collectives  44.3 us (21%)
  between operations  14.2 us (7%)
  Pallas kernels  10.7 us (5%)
  local copies, waits for them, and re-layouts  7.74 us (4%)
  other arithmetic  3.95 us (2%)
    all_to_all x4, waiting for transfers between devices, exchange(): return lax.all_to_all(pieces, axes, 0, 0, tiled=True)  44.3 us
    all_to_all x2, blocking collectives, exchange(): return lax.all_to_all(pieces, axes, 0, 0, tiled=True)  38.2 us
    all_to_all x4, starting transfers between devices, exchange(): return lax.all_to_all(pieces, axes, 0, 0, tiled=True)  29.7 us
    ppermute x1, waiting for transfers between devices, local(): other = lax.ppermute(mine, 'zh', [(0, 1), (1, 0)])  14.4 us
    ppermute x1, waiting for transfers between devices, local(): after_part = lax.ppermute(around[2], VOX, down)  14.1 us
    ppermute x1, starting transfers between devices, local(): before = lax.ppermute(ups, VOX, up)  13.9 us
    pallas_call x1, Pallas kernels, filter_grad(): pl.pallas_call(filter_kernel, grid=(runs,), in_specs=[pl.BlockSpec((cores...  4.38 us
  transfers between devices with their start and end apart: 11, of which 6 were waited for; matrix products, arithmetic and copies ran while one was open for 3% of the time, Pallas kernels for 4%

profile of v6, /device:TPU:47, one launch (start us, length us, event | category | flops | bytes accessed | tf_op | source)
XLA Modules:
  0.0 211.0 jit_solution(9394964848782064256)
XLA Ops:
  7.2 2.5 %collective-permute-start.3 = (bf16[32,512]{1,0:T(8,128)(2,1)}, bf16[32,512]{1,0:T(8,128)(2,1)S(1)}, u32[]{:S(2)}, u32[]{:S(2)}) collective-permute-start(bf16[32,512]{1,0:T(8,128)(2,1)} %bitcast.40), channel_id=1, source_target_pairs={{16,0},{32,16},{48,32},{64,48},{80,64},{96,80},{112,96},{128,112},... | collective-permute-start | bytes 98312 | tf_op jit(solution)/shard_map/ppermute | solution.py:215
  9.7 13.9 %collective-permute-start.2 = (bf16[32,512]{1,0:T(8,128)(2,1)}, bf16[32,512]{1,0:T(8,128)(2,1)S(1)}, u32[]{:S(2)}, u32[]{:S(2)}) collective-permute-start(bf16[32,512]{1,0:T(8,128)(2,1)} %bitcast.41), channel_id=1, source_target_pairs={{0,16},{16,32},{32,48},{48,64},{64,80},{80,96},{96,112},{112,128},... | collective-permute-start | bytes 98312 | tf_op jit(solution)/shard_map/ppermute | solution.py:214
  25.7 1.5 copy-done
  27.2 2.9 %backward_plane.1 = f32[2,8,64,512]{3,2,1,0:T(8,128)} custom-call(bf16[864,1024]{1,0:T(8,128)(2,1)S(1)} %bitcast.32, bf16[3,32,512]{2,1,0:T(8,128)(2,1)S(1)} %pad_maximum_fusion.1.u_ref), custom_call_target="tpu_custom_call" | custom-call | tf_op jit(solution)/shard_map/backward_plane/pallas_call | solution.py:85
  31.7 11.8 %all-to-all-start = ((bf16[8,64,512]{2,1,0:T(8,128)(2,1)}), bf16[8,64,512]{2,1,0:T(8,128)(2,1)S(1)}, u32[]{:S(2)}, u32[]{:S(2)}) async-start(bf16[8,64,512]{2,1,0:T(8,128)(2,1)} %broadcast_in_dim.15), calls=%async_computation | async-start | bytes 1048576 | tf_op jit(solution)/shard_map/all_to_all | solution.py:197
  43.5 25.6 %all-to-all-done = bf16[8,64,512]{2,1,0:T(8,128)(2,1)S(1)} async-done(((bf16[8,64,512]{2,1,0:T(8,128)(2,1)}), bf16[8,64,512]{2,1,0:T(8,128)(2,1)S(1)}, u32[]{:S(2)}, u32[]{:S(2)}) %all-to-all-start) | async-done | bytes 524320 | tf_op jit(solution)/shard_map/all_to_all | solution.py:197
  70.0 30.0 %all_to_all.30.u_ref = bf16[16,96,512]{2,1,0:T(8,128)(2,1)S(1)} all-to-all(bf16[16,96,512]{2,1,0:T(8,128)(2,1)S(1)} %pad_maximum_fusion), channel_id=1, replica_groups=mesh['y'=4,'zh'=2,'x'=4,'zl'=8,'co'=2] {'y','x'}, dimensions={0} | all-to-all | bytes 3145728 | tf_op jit(solution)/shard_map/all_to_all | solution.py:197
  100.1 8.2 %all_to_all.31.a_ref = bf16[2,16,32,512]{3,2,1,0:T(8,128)(2,1)S(1)} all-to-all(bf16[2,16,32,512]{3,2,1,0:T(8,128)(2,1)S(1)} %broadcast_in_dim.17), channel_id=1, replica_groups=mesh['y'=4,'zh'=2,'x'=4,'zl'=8,'co'=2] {'co'}, dimensions={0} | all-to-all | bytes 2097152 | tf_op jit(solution)/shard_map/all_to_all | solution.py:197
  108.3 4.4 %filter_planes.1 = f32[2,27,8,128]{3,2,1,0:T(8,128)} custom-call(bf16[2,16,32,512]{3,2,1,0:T(8,128)(2,1)S(1)} %all_to_all.31.a_ref, bf16[16,96,512]{2,1,0:T(8,128)(2,1)S(1)} %all_to_all.30.u_ref), custom_call_target="tpu_custom_call" | custom-call | tf_op jit(solution)/shard_map/filter_planes/pallas_call | solution.py:146
  112.7 4.5 %all-to-all-start.3 = ((f32[2,27,8,128]{3,2,1,0:T(8,128)}), f32[2,27,8,128]{3,2,1,0:T(8,128)S(1)}, u32[]{:S(2)}, u32[]{:S(2)}) async-start(f32[2,27,8,128]{3,2,1,0:T(8,128)} %filter_planes.1), calls=%async_computation.5 | async-start | bytes 442368 | tf_op jit(solution)/shard_map/all_to_all | solution.py:197
  117.9 18.7 %all-to-all-done.3 = f32[2,27,8,128]{3,2,1,0:T(8,128)S(1)} async-done(((f32[2,27,8,128]{3,2,1,0:T(8,128)}), f32[2,27,8,128]{3,2,1,0:T(8,128)S(1)}, u32[]{:S(2)}, u32[]{:S(2)}) %all-to-all-start.3) | async-done | bytes 221216 | tf_op jit(solution)/shard_map/all_to_all | solution.py:197
  137.7 6.8 %all-to-all-start.4 = ((bf16[16,27,8,128]{3,2,1,0:T(8,128)(2,1)}), bf16[16,27,8,128]{3,2,1,0:T(8,128)(2,1)S(1)}, u32[]{:S(2)}, u32[]{:S(2)}) async-start(bf16[16,27,8,128]{3,2,1,0:T(8,128)(2,1)} %broadcast_in_dim.18), calls=%async_computation.6 | async-start | bytes 1769472 | tf_op jit(solution)/shard_map/all_to_all | solution.py:197
  144.5 2.0 collective-permute-start.4
  146.5 14.4 %collective-permute-done.4 = bf16[27,8,128]{2,1,0:T(8,128)(2,1)S(1)} collective-permute-done((bf16[27,8,128]{2,1,0:T(8,128)(2,1)S(1)}, bf16[27,8,128]{2,1,0:T(8,128)(2,1)S(1)}, u32[]{:S(2)}, u32[]{:S(2)}) %collective-permute-start.4) | collective-permute-done | bytes 55328 | tf_op jit(solution)/shard_map/ppermute | solution.py:245
  161.9 6.6 %all-to-all-start.5 = ((bf16[16,27,8,128]{3,2,1,0:T(8,128)(2,1)}), bf16[16,27,8,128]{3,2,1,0:T(8,128)(2,1)S(1)}, u32[]{:S(2)}, u32[]{:S(2)}) async-start(bf16[16,27,8,128]{3,2,1,0:T(8,128)(2,1)} %broadcast_in_dim.19), calls=%async_computation.7 | async-start | bytes 1769472 | tf_op jit(solution)/shard_map/all_to_all | solution.py:197
  169.5 3.9 %all-gather = bf16[16,32,512]{2,1,0:T(8,128)(2,1)S(1)} all-gather(bf16[8,32,512]{2,1,0:T(8,128)(2,1)S(1)} %get-tuple-element.4), channel_id=2, replica_groups=mesh['y'=4,'zh'=2,'x'=4,'zl'=8,'co'=2] {'co'}, dimensions={0}, use_global_device_ids=true | all-gather | bytes 786432 | tf_op jit(solution)/shard_map/all_gather | solution.py:230
  173.5 2.2 %all-gather.1 = bf16[16,32,512]{2,1,0:T(8,128)(2,1)S(1)} all-gather(bf16[8,32,512]{2,1,0:T(8,128)(2,1)S(1)} %get-tuple-element.3), channel_id=3, replica_groups=mesh['y'=4,'zh'=2,'x'=4,'zl'=8,'co'=2] {'co'}, dimensions={0}, use_global_device_ids=true | all-gather | bytes 786432 | tf_op jit(solution)/shard_map/all_gather | solution.py:231
  177.6 2.2 %collective-permute-start.1 = (f32[32,512]{1,0:T(8,128)S(1)}, f32[32,512]{1,0:T(8,128)S(1)}, u32[]{:S(2)}, u32[]{:S(2)}) collective-permute-start(f32[32,512]{1,0:T(8,128)S(1)} %get-tuple-element.6), channel_id=1, source_target_pairs={{0,16},{16,32},{32,48},{48,64},{64,80},{80,96},{96,112},{112,128},... | collective-permute-start | bytes 196616 | tf_op jit(solution)/shard_map/ppermute | solution.py:234
  179.8 3.1 %collective-permute-start = (f32[32,512]{1,0:T(8,128)S(1)}, f32[32,512]{1,0:T(8,128)S(1)}, u32[]{:S(2)}, u32[]{:S(2)}) collective-permute-start(f32[32,512]{1,0:T(8,128)S(1)} %get-tuple-element.5), channel_id=1, source_target_pairs={{16,0},{32,16},{48,32},{64,48},{80,64},{96,80},{112,96},{128,112},... | collective-permute-start | bytes 196616 | tf_op jit(solution)/shard_map/ppermute | solution.py:233
  182.9 1.9 collective-permute-done.1
  184.7 14.1 %collective-permute-done = f32[32,512]{1,0:T(8,128)S(1)} collective-permute-done((f32[32,512]{1,0:T(8,128)S(1)}, f32[32,512]{1,0:T(8,128)S(1)}, u32[]{:S(2)}, u32[]{:S(2)}) %collective-permute-start) | collective-permute-done | bytes 65568 | tf_op jit(solution)/shard_map/ppermute | solution.py:233
  198.8 1.5 fusion.3
  200.3 2.3 %join_pieces.1 = bf16[27,32,1024]{2,1,0:T(8,128)(2,1)} custom-call(s32[1]{0:T(128)} %bitcast.16.own_ref, bf16[16,27,8,128]{3,2,1,0:T(8,128)(2,1)S(1)} %all-to-all-done.4.a_ref, bf16[16,27,8,128]{3,2,1,0:T(8,128)(2,1)S(1)} %all-to-all-done.5.b_ref), custom_call_target="tpu_custom_call" | custom-call | tf_op jit(solution)/shard_map/join_pieces/pallas_call | solution.py:182
  202.6 1.5 convert_bitcast_fusion
  (36 shorter events, 10.5 us)
Async XLA Ops:
  7.2 110.0 %reduce-scatter.3.cloned.1.call-start = ((), (), s32[]{:S(2)}) async-start(), calls=%async_computation.8 | async-start | bytes 3145728 | tf_op jit(solution)/shard_map/reduce_scatter | solution.py:221
  7.2 16.4 %collective-permute-start.3 = (bf16[32,512]{1,0:T(8,128)(2,1)}, bf16[32,512]{1,0:T(8,128)(2,1)S(1)}, u32[]{:S(2)}, u32[]{:S(2)}) collective-permute-start(bf16[32,512]{1,0:T(8,128)(2,1)} %bitcast.40), channel_id=1, source_target_pairs={{16,0},{32,16},{48,32},{64,48},{80,64},{96,80},{112,96},{128,112},... | collective-permute-start | bytes 98312 | tf_op jit(solution)/shard_map/ppermute | solution.py:215
  9.7 15.2 %collective-permute-start.2 = (bf16[32,512]{1,0:T(8,128)(2,1)}, bf16[32,512]{1,0:T(8,128)(2,1)S(1)}, u32[]{:S(2)}, u32[]{:S(2)}) collective-permute-start(bf16[32,512]{1,0:T(8,128)(2,1)} %bitcast.41), channel_id=1, source_target_pairs={{0,16},{16,32},{32,48},{48,64},{64,80},{80,96},{96,112},{112,128},... | collective-permute-start | bytes 98312 | tf_op jit(solution)/shard_map/ppermute | solution.py:214
  25.7 1.5 copy-start
  30.0 0.8 copy-start.5
  30.1 13.5 %copy-start.4 = (bf16[32,1,512]{2,0,1:T(8,128)(2,1)S(1)}, bf16[32,1,512]{2,0,1:T(8,128)(2,1)}, u32[]{:S(2)}) copy-start(bf16[32,1,512]{2,0,1:T(8,128)(2,1)} %param.4) | copy-start | bytes 98308
  31.7 37.4 %all-to-all-start = ((bf16[8,64,512]{2,1,0:T(8,128)(2,1)}), bf16[8,64,512]{2,1,0:T(8,128)(2,1)S(1)}, u32[]{:S(2)}, u32[]{:S(2)}) async-start(bf16[8,64,512]{2,1,0:T(8,128)(2,1)} %broadcast_in_dim.15), calls=%async_computation | async-start | bytes 1048576 | tf_op jit(solution)/shard_map/all_to_all | solution.py:197
  69.2 0.8 copy-start.3
  112.7 23.9 %all-to-all-start.3 = ((f32[2,27,8,128]{3,2,1,0:T(8,128)}), f32[2,27,8,128]{3,2,1,0:T(8,128)S(1)}, u32[]{:S(2)}, u32[]{:S(2)}) async-start(f32[2,27,8,128]{3,2,1,0:T(8,128)} %filter_planes.1), calls=%async_computation.5 | async-start | bytes 442368 | tf_op jit(solution)/shard_map/all_to_all | solution.py:197
  117.2 85.4 %reduce-scatter.5.cloned.1.call-start = ((), (), s32[]{:S(2)}) async-start(), calls=%async_computation.9 | async-start | bytes 1179648 | tf_op jit(solution)/shard_map/reduce_scatter | solution.py:222
  137.7 23.2 %all-to-all-start.4 = ((bf16[16,27,8,128]{3,2,1,0:T(8,128)(2,1)}), bf16[16,27,8,128]{3,2,1,0:T(8,128)(2,1)S(1)}, u32[]{:S(2)}, u32[]{:S(2)}) async-start(bf16[16,27,8,128]{3,2,1,0:T(8,128)(2,1)} %broadcast_in_dim.18), calls=%async_computation.6 | async-start | bytes 1769472 | tf_op jit(solution)/shard_map/all_to_all | solution.py:197
  144.5 16.3 %collective-permute-start.4 = (bf16[27,8,128]{2,1,0:T(8,128)(2,1)S(1)}, bf16[27,8,128]{2,1,0:T(8,128)(2,1)S(1)}, u32[]{:S(2)}, u32[]{:S(2)}) collective-permute-start(bf16[27,8,128]{2,1,0:T(8,128)(2,1)S(1)} %multiply_convert_fusion), channel_id=1, source_target_pairs={{0,64},{64,0},{1,65},{65,1},{2,66},{66,2},{3,67},{67,3},{4,68},{68... | collective-permute-start | bytes 165896 | tf_op jit(solution)/shard_map/ppermute | solution.py:245
  161.9 13.8 %copy-start.1 = (bf16[32,27,1024]{2,0,1:T(8,128)(2,1)S(1)}, bf16[32,27,1024]{2,0,1:T(8,128)(2,1)}, u32[]{:S(2)}) copy-start(bf16[32,27,1024]{2,0,1:T(8,128)(2,1)} %param.5) | copy-start | bytes 5308420
  161.9 38.4 %all-to-all-start.5 = ((bf16[16,27,8,128]{3,2,1,0:T(8,128)(2,1)}), bf16[16,27,8,128]{3,2,1,0:T(8,128)(2,1)S(1)}, u32[]{:S(2)}, u32[]{:S(2)}) async-start(bf16[16,27,8,128]{3,2,1,0:T(8,128)(2,1)} %broadcast_in_dim.19), calls=%async_computation.7 | async-start | bytes 1769472 | tf_op jit(solution)/shard_map/all_to_all | solution.py:197
  176.9 0.7 copy-start.2
  177.6 7.2 %collective-permute-start.1 = (f32[32,512]{1,0:T(8,128)S(1)}, f32[32,512]{1,0:T(8,128)S(1)}, u32[]{:S(2)}, u32[]{:S(2)}) collective-permute-start(f32[32,512]{1,0:T(8,128)S(1)} %get-tuple-element.6), channel_id=1, source_target_pairs={{0,16},{16,32},{32,48},{48,64},{64,80},{80,96},{96,112},{112,128},... | collective-permute-start | bytes 196616 | tf_op jit(solution)/shard_map/ppermute | solution.py:234
  179.8 19.1 %collective-permute-start = (f32[32,512]{1,0:T(8,128)S(1)}, f32[32,512]{1,0:T(8,128)S(1)}, u32[]{:S(2)}, u32[]{:S(2)}) collective-permute-start(f32[32,512]{1,0:T(8,128)S(1)} %get-tuple-element.5), channel_id=1, source_target_pairs={{16,0},{32,16},{48,32},{64,48},{80,64},{96,80},{112,96},{128,112},... | collective-permute-start | bytes 196616 | tf_op jit(solution)/shard_map/ppermute | solution.py:233
Sparse Core Ops, SparseCore 0:
  30.2 30.0 reduce-scatter.2
  120.8 60.1 reduce-scatter.4

commit v7 on v5

--- a/solution.py
+++ b/solution.py
@@ -13,6 +13,7 @@
 VOX = ("y", "zh", "x")
 XY = ("y", "x")
 CHAN = ("zl", "co")
+RING = ("zh", "zl")
 F32 = jnp.float32
 BF16 = jnp.bfloat16
 
@@ -231,8 +232,16 @@
 
     acts = shared(mixed[:, : cin // (2 * n_xy)], "co")
     raw = filter_grad(acts, mixed, n_y)
-    raw = exchange(raw, "zh")
-    raw = jnp.sum(raw, axis=0)
+    side = lax.axis_index("zh")
+    swapped = exchange(raw[:, :18], "zh")
+    n_z = lax.axis_size(RING)
+    back = [(i, (i - n_z // 4) % n_z) for i in range(n_z)]
+    kept = jnp.where(side == 0, raw[0, 18:], raw[1, 18:])
+    sent = jnp.where(side == 0, raw[1, 18:], raw[0, 18:])
+    sent = lax.ppermute(sent, RING, back)
+    sent = lax.ppermute(sent, RING, back)
+    swapped = jnp.sum(swapped, axis=0)
+    raw = jnp.concatenate([swapped, kept + sent])
     scale = 1.0 / jnp.sqrt(jnp.float32(n_vox * PLANE))
     mine = (raw * scale).astype(BF16)
     halves = shared(mine, "zh")

time: 208 us -> 213 us (1.024)
  the two profiles are of different devices: /device:TPU:6 before, /device:TPU:39 now
where the time goes in v7:
time: 213 us; the launch traced here: 212 us
  starting transfers between devices  73.2 us (34%)
  waiting for transfers between devices  68.3 us (32%)
  blocking collectives  36.8 us (17%)
  between operations  14.2 us (7%)
  Pallas kernels  10.1 us (5%)
  local copies, waits for them, and re-layouts  5.54 us (3%)
  other arithmetic  4.29 us (2%)
    all_to_all x4, waiting for transfers between devices, exchange(): return lax.all_to_all(pieces, axes, 0, 0, tiled=True)  45.9 us
    all_to_all x4, starting transfers between devices, exchange(): return lax.all_to_all(pieces, axes, 0, 0, tiled=True)  39 us
    all_to_all x2, blocking collectives, exchange(): return lax.all_to_all(pieces, axes, 0, 0, tiled=True)  27.4 us
    ppermute x1, waiting for transfers between devices, local(): after_part = lax.ppermute(around[2], VOX, down)  18.7 us
    ppermute x1, starting transfers between devices, local(): before = lax.ppermute(ups, VOX, up)  13.9 us
    ppermute x2, starting transfers between devices, local(): sent = lax.ppermute(sent, RING, back)  12.5 us
    all_gather x1, blocking collectives, local(): low = lax.all_gather(near[:, :ch // 2], 'co', axis=0, tiled=False)  7.22 us
  transfers between devices with their start and end apart: 12, of which 8 were waited for; matrix products, arithmetic and copies ran while one was open for 2% of the time, Pallas kernels for 3%

profile of v7, /device:TPU:39, one launch (start us, length us, event | category | flops | bytes accessed | tf_op | source)
XLA Modules:
  0.0 212.5 jit_solution(3498436638345091964)
XLA Ops:
  7.2 2.5 %collective-permute-start.3 = (bf16[32,512]{1,0:T(8,128)(2,1)}, bf16[32,512]{1,0:T(8,128)(2,1)S(1)}, u32[]{:S(2)}, u32[]{:S(2)}) collective-permute-start(bf16[32,512]{1,0:T(8,128)(2,1)} %bitcast.43), channel_id=1, source_target_pairs={{16,0},{32,16},{48,32},{64,48},{80,64},{96,80},{112,96},{128,112},... | collective-permute-start | bytes 98312 | tf_op jit(solution)/shard_map/ppermute | solution.py:211
  9.7 13.9 %collective-permute-start.2 = (bf16[32,512]{1,0:T(8,128)(2,1)}, bf16[32,512]{1,0:T(8,128)(2,1)S(1)}, u32[]{:S(2)}, u32[]{:S(2)}) collective-permute-start(bf16[32,512]{1,0:T(8,128)(2,1)} %bitcast.44), channel_id=1, source_target_pairs={{0,16},{16,32},{32,48},{48,64},{64,80},{80,96},{96,112},{112,128},... | collective-permute-start | bytes 98312 | tf_op jit(solution)/shard_map/ppermute | solution.py:210
  23.6 1.3 collective-permute-done.2
  25.7 1.5 copy-done
  27.2 2.9 %backward_plane.1 = f32[2,8,64,512]{3,2,1,0:T(8,128)} custom-call(bf16[864,1024]{1,0:T(8,128)(2,1)S(1)} %bitcast.35, bf16[3,32,512]{2,1,0:T(8,128)(2,1)S(1)} %pad_maximum_fusion.1.u_ref), custom_call_target="tpu_custom_call" | custom-call | tf_op jit(solution)/shard_map/backward_plane/pallas_call | solution.py:86
  31.7 11.8 %all-to-all-start = ((bf16[8,64,512]{2,1,0:T(8,128)(2,1)}), bf16[8,64,512]{2,1,0:T(8,128)(2,1)S(1)}, u32[]{:S(2)}, u32[]{:S(2)}) async-start(bf16[8,64,512]{2,1,0:T(8,128)(2,1)} %broadcast_in_dim.15), calls=%async_computation | async-start | bytes 1048576 | tf_op jit(solution)/shard_map/all_to_all | solution.py:193
  43.6 25.6 %all-to-all-done = bf16[8,64,512]{2,1,0:T(8,128)(2,1)S(1)} async-done(((bf16[8,64,512]{2,1,0:T(8,128)(2,1)}), bf16[8,64,512]{2,1,0:T(8,128)(2,1)S(1)}, u32[]{:S(2)}, u32[]{:S(2)}) %all-to-all-start) | async-done | bytes 524320 | tf_op jit(solution)/shard_map/all_to_all | solution.py:193
  70.6 13.7 %all-to-all-start.1 = ((bf16[16,96,512]{2,1,0:T(8,128)(2,1)}), bf16[16,96,512]{2,1,0:T(8,128)(2,1)S(1)}, u32[]{:S(2)}, u32[]{:S(2)}) async-start(bf16[16,96,512]{2,1,0:T(8,128)(2,1)} %pad_maximum_fusion), calls=%async_computation.3 | async-start | bytes 3145728 | tf_op jit(solution)/shard_map/all_to_all | solution.py:193
  84.3 20.0 %all-to-all-done.1.u_ref = bf16[16,96,512]{2,1,0:T(8,128)(2,1)S(1)} async-done(((bf16[16,96,512]{2,1,0:T(8,128)(2,1)}), bf16[16,96,512]{2,1,0:T(8,128)(2,1)S(1)}, u32[]{:S(2)}, u32[]{:S(2)}) %all-to-all-start.1) | async-done | bytes 1572896 | tf_op jit(solution)/shard_map/all_to_all | solution.py:193
  104.4 5.6 %all_to_all.30.a_ref = bf16[2,16,32,512]{3,2,1,0:T(8,128)(2,1)S(1)} all-to-all(bf16[2,16,32,512]{3,2,1,0:T(8,128)(2,1)S(1)} %broadcast_in_dim.17), channel_id=1, replica_groups=mesh['y'=4,'zh'=2,'x'=4,'zl'=8,'co'=2] {'co'}, dimensions={0} | all-to-all | bytes 2097152 | tf_op jit(solution)/shard_map/all_to_all | solution.py:193
  110.0 3.7 %filter_planes.1 = f32[2,27,8,128]{3,2,1,0:T(8,128)S(1)} custom-call(bf16[2,16,32,512]{3,2,1,0:T(8,128)(2,1)S(1)} %all_to_all.30.a_ref, bf16[16,96,512]{2,1,0:T(8,128)(2,1)S(1)} %all-to-all-done.1.u_ref), custom_call_target="tpu_custom_call" | custom-call | tf_op jit(solution)/shard_map/filter_planes/pallas_call | solution.py:147
  113.8 1.9 collective-permute-start.4
  116.4 6.0 %all-to-all-start.3 = ((f32[2,18,8,128]{3,2,1,0:T(8,128)}), f32[2,18,8,128]{3,2,1,0:T(8,128)S(1)}, u32[]{:S(2)}, u32[]{:S(2)}) async-start(f32[2,18,8,128]{3,2,1,0:T(8,128)} %slice.44), calls=%async_computation.5 | async-start | bytes 294912 | tf_op jit(solution)/shard_map/all_to_all | solution.py:193
  122.6 10.6 %collective-permute-start.5 = (f32[9,8,128]{2,1,0:T(8,128)S(1)}, f32[9,8,128]{2,1,0:T(8,128)S(1)}, u32[]{:S(2)}, u32[]{:S(2)}) collective-permute-start(f32[9,8,128]{2,1,0:T(8,128)S(1)} %collective-permute-done.4), channel_id=1, source_target_pairs={{0,72},{2,74},{4,76},{6,78},{8,0},{10,2},{12,4},{14,6},{64,8},{66,... | collective-permute-start | bytes 110600 | tf_op jit(solution)/shard_map/ppermute | solution.py:242
  134.7 21.8 %all_to_all.31 = bf16[2,27,8,128]{3,2,1,0:T(8,128)(2,1)S(1)} all-to-all(bf16[2,27,8,128]{3,2,1,0:T(8,128)(2,1)S(1)} %broadcast_in_dim.18), channel_id=1, replica_groups=mesh['y'=4,'zh'=2,'x'=4,'zl'=8,'co'=2] {'zh'}, dimensions={0} | all-to-all | bytes 221184 | tf_op jit(solution)/shard_map/all_to_all | solution.py:193
  156.5 1.4 broadcast_in_dim.19
  157.9 7.5 %all-to-all-start.5 = ((bf16[16,2,27,8,128]{4,3,2,1,0:T(8,128)(2,1)}), bf16[16,2,27,8,128]{4,3,2,1,0:T(8,128)(2,1)S(1)}, u32[]{:S(2)}, u32[]{:S(2)}) async-start(bf16[16,2,27,8,128]{4,3,2,1,0:T(8,128)(2,1)} %broadcast_in_dim.19), calls=%async_computation.7 | async-start | bytes 3538944 | tf_op jit(solution)/shard_map/all_to_all | solution.py:193
  165.4 7.2 %all-gather = bf16[16,32,512]{2,1,0:T(8,128)(2,1)S(1)} all-gather(bf16[8,32,512]{2,1,0:T(8,128)(2,1)S(1)} %get-tuple-element.4), channel_id=2, replica_groups=mesh['y'=4,'zh'=2,'x'=4,'zl'=8,'co'=2] {'co'}, dimensions={0}, use_global_device_ids=true | all-gather | bytes 786432 | tf_op jit(solution)/shard_map/all_gather | solution.py:226
  172.7 2.2 %all-gather.1 = bf16[16,32,512]{2,1,0:T(8,128)(2,1)S(1)} all-gather(bf16[8,32,512]{2,1,0:T(8,128)(2,1)S(1)} %get-tuple-element.3), channel_id=3, replica_groups=mesh['y'=4,'zh'=2,'x'=4,'zl'=8,'co'=2] {'co'}, dimensions={0}, use_global_device_ids=true | all-gather | bytes 786432 | tf_op jit(solution)/shard_map/all_gather | solution.py:227
  176.1 1.9 collective-permute-start.1
  178.0 3.4 %collective-permute-start = (f32[32,512]{1,0:T(8,128)S(1)}, f32[32,512]{1,0:T(8,128)S(1)}, u32[]{:S(2)}, u32[]{:S(2)}) collective-permute-start(f32[32,512]{1,0:T(8,128)S(1)} %get-tuple-element.5), channel_id=1, source_target_pairs={{16,0},{32,16},{48,32},{64,48},{80,64},{96,80},{112,96},{128,112},... | collective-permute-start | bytes 196616 | tf_op jit(solution)/shard_map/ppermute | solution.py:229
  182.5 18.7 %collective-permute-done = f32[32,512]{1,0:T(8,128)S(1)} collective-permute-done((f32[32,512]{1,0:T(8,128)S(1)}, f32[32,512]{1,0:T(8,128)S(1)}, u32[]{:S(2)}, u32[]{:S(2)}) %collective-permute-start) | collective-permute-done | bytes 65568 | tf_op jit(solution)/shard_map/ppermute | solution.py:229
  201.8 2.3 %join_pieces.1 = bf16[27,32,1024]{2,1,0:T(8,128)(2,1)} custom-call(bf16[16,2,27,8,128]{4,3,2,1,0:T(8,128)(2,1)S(1)} %all-to-all-done.5.r_ref), custom_call_target="tpu_custom_call" | custom-call | tf_op jit(solution)/shard_map/join_pieces/pallas_call | solution.py:181
  204.1 1.5 convert_bitcast_fusion
  (37 shorter events, 9.4 us)
Async XLA Ops:
  7.2 126.1 %reduce-scatter.3.cloned.1.call-start = ((), (), s32[]{:S(2)}) async-start(), calls=%async_computation.8 | async-start | bytes 3145728 | tf_op jit(solution)/shard_map/reduce_scatter | solution.py:217
  7.2 16.4 %collective-permute-start.3 = (bf16[32,512]{1,0:T(8,128)(2,1)}, bf16[32,512]{1,0:T(8,128)(2,1)S(1)}, u32[]{:S(2)}, u32[]{:S(2)}) collective-permute-start(bf16[32,512]{1,0:T(8,128)(2,1)} %bitcast.43), channel_id=1, source_target_pairs={{16,0},{32,16},{48,32},{64,48},{80,64},{96,80},{112,96},{128,112},... | collective-permute-start | bytes 98312 | tf_op jit(solution)/shard_map/ppermute | solution.py:211
  9.7 15.2 %collective-permute-start.2 = (bf16[32,512]{1,0:T(8,128)(2,1)}, bf16[32,512]{1,0:T(8,128)(2,1)S(1)}, u32[]{:S(2)}, u32[]{:S(2)}) collective-permute-start(bf16[32,512]{1,0:T(8,128)(2,1)} %bitcast.44), channel_id=1, source_target_pairs={{0,16},{16,32},{32,48},{48,64},{64,80},{80,96},{96,112},{112,128},... | collective-permute-start | bytes 98312 | tf_op jit(solution)/shard_map/ppermute | solution.py:210
  25.7 1.5 copy-start
  30.1 0.8 copy-start.3
  30.1 13.5 %copy-start.2 = (bf16[32,1,512]{2,0,1:T(8,128)(2,1)S(1)}, bf16[32,1,512]{2,0,1:T(8,128)(2,1)}, u32[]{:S(2)}) copy-start(bf16[32,1,512]{2,0,1:T(8,128)(2,1)} %param.4) | copy-start | bytes 98308
  31.7 37.5 %all-to-all-start = ((bf16[8,64,512]{2,1,0:T(8,128)(2,1)}), bf16[8,64,512]{2,1,0:T(8,128)(2,1)S(1)}, u32[]{:S(2)}, u32[]{:S(2)}) async-start(bf16[8,64,512]{2,1,0:T(8,128)(2,1)} %broadcast_in_dim.15), calls=%async_computation | async-start | bytes 1048576 | tf_op jit(solution)/shard_map/all_to_all | solution.py:193
  70.6 33.7 %all-to-all-start.1 = ((bf16[16,96,512]{2,1,0:T(8,128)(2,1)}), bf16[16,96,512]{2,1,0:T(8,128)(2,1)S(1)}, u32[]{:S(2)}, u32[]{:S(2)}) async-start(bf16[16,96,512]{2,1,0:T(8,128)(2,1)} %pad_maximum_fusion), calls=%async_computation.3 | async-start | bytes 3145728 | tf_op jit(solution)/shard_map/all_to_all | solution.py:193
  113.8 8.9 %collective-permute-start.4 = (f32[9,8,128]{2,1,0:T(8,128)S(1)}, f32[9,8,128]{2,1,0:T(8,128)S(1)}, u32[]{:S(2)}, u32[]{:S(2)}) collective-permute-start(f32[9,8,128]{2,1,0:T(8,128)S(1)} %select_bitcast_fusion), channel_id=1, source_target_pairs={{0,72},{2,74},{4,76},{6,78},{8,0},{10,2},{12,4},{14,6},{64,8},{66,... | collective-permute-start | bytes 110600 | tf_op jit(solution)/shard_map/ppermute | solution.py:241
  116.4 18.2 %all-to-all-start.3 = ((f32[2,18,8,128]{3,2,1,0:T(8,128)}), f32[2,18,8,128]{3,2,1,0:T(8,128)S(1)}, u32[]{:S(2)}, u32[]{:S(2)}) async-start(f32[2,18,8,128]{3,2,1,0:T(8,128)} %slice.44), calls=%async_computation.5 | async-start | bytes 294912 | tf_op jit(solution)/shard_map/all_to_all | solution.py:193
  122.4 81.7 %reduce-scatter.5.cloned.1.call-start = ((), (), s32[]{:S(2)}) async-start(), calls=%async_computation.9 | async-start | bytes 1179648 | tf_op jit(solution)/shard_map/reduce_scatter | solution.py:218
  122.6 11.6 %collective-permute-start.5 = (f32[9,8,128]{2,1,0:T(8,128)S(1)}, f32[9,8,128]{2,1,0:T(8,128)S(1)}, u32[]{:S(2)}, u32[]{:S(2)}) collective-permute-start(f32[9,8,128]{2,1,0:T(8,128)S(1)} %collective-permute-done.4), channel_id=1, source_target_pairs={{0,72},{2,74},{4,76},{6,78},{8,0},{10,2},{12,4},{14,6},{64,8},{66,... | collective-permute-start | bytes 110600 | tf_op jit(solution)/shard_map/ppermute | solution.py:242
  157.9 43.9 %all-to-all-start.5 = ((bf16[16,2,27,8,128]{4,3,2,1,0:T(8,128)(2,1)}), bf16[16,2,27,8,128]{4,3,2,1,0:T(8,128)(2,1)S(1)}, u32[]{:S(2)}, u32[]{:S(2)}) async-start(bf16[16,2,27,8,128]{4,3,2,1,0:T(8,128)(2,1)} %broadcast_in_dim.19), calls=%async_computation.7 | async-start | bytes 3538944 | tf_op jit(solution)/shard_map/all_to_all | solution.py:193
  165.4 9.4 %copy-start.1 = (bf16[32,27,1024]{2,0,1:T(8,128)(2,1)S(1)}, bf16[32,27,1024]{2,0,1:T(8,128)(2,1)}, u32[]{:S(2)}) copy-start(bf16[32,27,1024]{2,0,1:T(8,128)(2,1)} %param.5) | copy-start | bytes 5308420
  176.1 6.4 %collective-permute-start.1 = (f32[32,512]{1,0:T(8,128)S(1)}, f32[32,512]{1,0:T(8,128)S(1)}, u32[]{:S(2)}, u32[]{:S(2)}) collective-permute-start(f32[32,512]{1,0:T(8,128)S(1)} %get-tuple-element.6), channel_id=1, source_target_pairs={{0,16},{16,32},{32,48},{48,64},{64,80},{80,96},{96,112},{112,128},... | collective-permute-start | bytes 196616 | tf_op jit(solution)/shard_map/ppermute | solution.py:230
  178.0 23.2 %collective-permute-start = (f32[32,512]{1,0:T(8,128)S(1)}, f32[32,512]{1,0:T(8,128)S(1)}, u32[]{:S(2)}, u32[]{:S(2)}) collective-permute-start(f32[32,512]{1,0:T(8,128)S(1)} %get-tuple-element.5), channel_id=1, source_target_pairs={{16,0},{32,16},{48,32},{64,48},{80,64},{96,80},{112,96},{128,112},... | collective-permute-start | bytes 196616 | tf_op jit(solution)/shard_map/ppermute | solution.py:229
Sparse Core Ops, SparseCore 0:
  30.2 30.1 reduce-scatter.2
  133.4 56.9 reduce-scatter.4
